TPU v7x, 256 devices: a whole 4x4x8 slice. The times are simulated.
256 devices in a mesh: frames: 32 (over z, x_lo, core), runs: 8 (over y, x_hi).
Axes of the slice: x: 4 (x_hi: 2, x_lo: 2; x = x_hi * 2 + x_lo), y: 4, z: 8, core: 2. Of those that a mesh axis runs over, the one named last changes fastest.
Arguments:
- inputs: bfloat16 [8, 131072, 256], P('runs', 'frames'), may hold values from -6 to 6
- first_layer_weight: bfloat16 [3, 256, 256], replicated, may hold values from -0.21875 to 0.21875
- first_layer_bias: bfloat16 [256], replicated, may hold values from -3 to 3
- second_layer_weight: bfloat16 [3, 256, 256], replicated, may hold values from -0.21875 to 0.21875
- second_layer_bias: bfloat16 [256], replicated, may hold values from -3 to 3
- upstream: bfloat16 [8, 131072, 256], P('runs', 'frames'), may hold values from -6 to 6
Outputs:
- outputs: bfloat16 [8, 131072, 256], P('runs', 'frames')
- grad_input: bfloat16 [8, 131072, 256], P('runs', 'frames')
- grad_w_first: float32 [3, 256, 256], replicated
- grad_b_first: float32 [256], replicated
- grad_w_second: float32 [3, 256, 256], replicated
- grad_b_second: float32 [256], replicated
All inputs are finite; a program needn't handle non-finite values.
Results may differ from a plain program's by a relative error of at most 0.007.
Values may be sent and summed in bfloat16 or wider, within the bound.
A program may use at most 128 MiB of HBM per device.

v0:
```python
import math

import jax
import jax.numpy as jnp
from jax import lax
from jax.sharding import PartitionSpec as P

FIRST_SPACING = 256
SECOND_SPACING = 512


def passed_along(block, axis, distance):
    devices = range(lax.axis_size(axis))
    route = [(i - distance, i) for i in devices if i - distance in devices]
    return lax.ppermute(block, axis, route)


def gelu_slope(pre, grad):
    return jax.vjp(jax.nn.gelu, pre)[1](grad)[0]


def causal_conv_apply(extended, weights, bias, dilation, frame_count):
    total = bias.astype(jnp.float32)[None, None, :]
    for k in range(3):
        start = 2 * dilation - k * dilation
        total = total + jnp.einsum(
            "rtc,cd->rtd",
            extended[:, start : start + frame_count],
            weights[k],
            preferred_element_type=jnp.float32,
        )
    return total


def causal_conv_weight_gradient(extended, grad, dilation, frame_count):
    pieces = []
    for k in range(3):
        start = 2 * dilation - k * dilation
        pieces.append(
            jnp.einsum(
                "rtc,rtd->cd",
                extended[:, start : start + frame_count],
                grad,
                preferred_element_type=jnp.float32,
            )
        )
    return jnp.stack(pieces)


def local_terms(grad, weights, dilation, frame_count):
    padded = jnp.pad(grad, ((0, 0), (0, 2 * dilation), (0, 0)))
    total = jnp.zeros(grad.shape, jnp.float32)
    for k in range(3):
        start = k * dilation
        total = total + jnp.einsum(
            "rtd,cd->rtc",
            padded[:, start : start + frame_count],
            weights[k],
            preferred_element_type=jnp.float32,
        )
    return total


def rim_terms(grad, weights, dilation):
    far_terms = jnp.einsum(
        "rtd,cd->rtc", grad[:, : 2 * dilation], weights[2], preferred_element_type=jnp.float32
    )
    near_terms = jnp.einsum(
        "rtd,cd->rtc", grad[:, :dilation], weights[1], preferred_element_type=jnp.float32
    )
    return far_terms + jnp.pad(near_terms, ((0, 0), (dilation, 0), (0, 0)))


def place_tail(arrived, frame_count, dilation):
    return jnp.pad(arrived, ((0, 0), (frame_count - 2 * dilation, 0), (0, 0)))


def causal_conv_input_gradient(grad, weights, dilation, frame_count, layer):
    total = local_terms(grad, weights, dilation, frame_count)
    rim_part = rim_terms(grad, weights, dilation)
    if layer == 2:
        arrived = passed_along(rim_part.astype(jnp.bfloat16), "frames", -1).astype(rim_part.dtype)
    else:
        arrived = passed_along(rim_part.astype(jnp.bfloat16), "frames", -1).astype(rim_part.dtype)
    return total + place_tail(arrived, frame_count, dilation)


def body(
    inputs, first_layer_weight, first_layer_bias, second_layer_weight, second_layer_bias, upstream
):
    frame_count = inputs.shape[1]
    prior_frames = passed_along(inputs[:, frame_count - 2 * FIRST_SPACING :], "frames", 1)
    input_with_history = jnp.concatenate([prior_frames, inputs], axis=1)
    first_preactivation = causal_conv_apply(
        input_with_history, first_layer_weight, first_layer_bias, FIRST_SPACING, frame_count
    )
    hidden_state = (inputs.astype(jnp.float32) + jax.nn.gelu(first_preactivation)).astype(
        jnp.bfloat16
    )
    prior_hidden_frames = passed_along(
        hidden_state[:, frame_count - 2 * SECOND_SPACING :], "frames", 1
    )
    hidden_with_history = jnp.concatenate([prior_hidden_frames, hidden_state], axis=1)
    second_preactivation = causal_conv_apply(
        hidden_with_history, second_layer_weight, second_layer_bias, SECOND_SPACING, frame_count
    )
    result = (hidden_state.astype(jnp.float32) + jax.nn.gelu(second_preactivation)).astype(
        jnp.bfloat16
    )
    output_gradient = upstream.astype(jnp.float32)
    second_layer_gradient = gelu_slope(second_preactivation, output_gradient).astype(jnp.bfloat16)
    second_weight_delta = causal_conv_weight_gradient(
        hidden_with_history, second_layer_gradient, SECOND_SPACING, frame_count
    )
    db_second = jnp.sum(second_layer_gradient.astype(jnp.float32), axis=(0, 1))
    hidden_gradient = output_gradient + causal_conv_input_gradient(
        second_layer_gradient, second_layer_weight, SECOND_SPACING, frame_count, 2
    )
    first_layer_gradient = gelu_slope(first_preactivation, hidden_gradient).astype(jnp.bfloat16)
    input_gradient_rows = (
        hidden_gradient
        + causal_conv_input_gradient(
            first_layer_gradient, first_layer_weight, FIRST_SPACING, frame_count, 1
        )
    ).astype(jnp.bfloat16)
    first_weight_delta = causal_conv_weight_gradient(
        input_with_history, first_layer_gradient, FIRST_SPACING, frame_count
    )
    db_first = jnp.sum(first_layer_gradient.astype(jnp.float32), axis=(0, 1))
    factor = 1.0 / math.sqrt(
        inputs.shape[0] * lax.axis_size("runs") * frame_count * lax.axis_size("frames")
    )
    sum_w_first, sum_b_first, sum_w_second, sum_b_second = lax.psum(
        (first_weight_delta, db_first, second_weight_delta, db_second), ("frames", "runs")
    )
    sum_w_first = sum_w_first * factor
    sum_b_first = sum_b_first * factor
    sum_w_second = sum_w_second * factor
    sum_b_second = sum_b_second * factor
    return (result, input_gradient_rows, sum_w_first, sum_b_first, sum_w_second, sum_b_second)


def solution(mesh):
    return jax.shard_map(
        body,
        mesh=mesh,
        in_specs=(P("runs", "frames", None), P(), P(), P(), P(), P("runs", "frames", None)),
        out_specs=(P("runs", "frames", None), P("runs", "frames", None), P(), P(), P(), P()),
        check_vma=False,
    )
```

profile of v0, /device:TPU:1, one launch (start us, length us, event | category | flops | bytes accessed | tf_op | source)
XLA Modules:
  0.0 346.2 jit_solution(14924929035905152933)
XLA Ops:
  7.2 1.0 slice.77
  8.2 4.5 %collective-permute-start = (bf16[1,512,256]{2,1,0:T(8,128)(2,1)S(1)}, bf16[1,512,256]{2,1,0:T(8,128)(2,1)S(1)}, u32[]{:S(2)}, u32[]{:S(2)}) collective-permute-start(bf16[1,512,256]{2,1,0:T(8,128)(2,1)S(1)} %slice.77), channel_id=1, source_target_pairs={{0,8},{8,16},{16,24},{24,32},{32,40},{40,48},{48,56},{56,64},{64,7... | collective-permute-start | bytes 786440 | tf_op jit(solution)/shard_map/ppermute | solution.py:15
  13.4 2.4 convolution_add_fusion.9
  17.6 1.9 fusion.24
  19.5 3.8 %collective-permute-start.1 = (bf16[1,1024,256]{2,1,0:T(8,128)(2,1)S(1)}, bf16[1,1024,256]{2,1,0:T(8,128)(2,1)S(1)}, u32[]{:S(2)}, u32[]{:S(2)}) collective-permute-start(bf16[1,1024,256]{2,1,0:T(8,128)(2,1)S(1)} %slice.98), channel_id=1, source_target_pairs={{0,8},{8,16},{16,24},{24,32},{32,40},{40,48},{48,56},{56,64},{64,7... | collective-permute-start | bytes 1572872 | tf_op jit(solution)/shard_map/ppermute | solution.py:15
  24.1 5.3 %collective-permute-done.1 = bf16[1,1024,256]{2,1,0:T(8,128)(2,1)S(1)} collective-permute-done((bf16[1,1024,256]{2,1,0:T(8,128)(2,1)S(1)}, bf16[1,1024,256]{2,1,0:T(8,128)(2,1)S(1)}, u32[]{:S(2)}, u32[]{:S(2)}) %collective-permute-start.1) | collective-permute-done | bytes 524320 | tf_op jit(solution)/shard_map/ppermute | solution.py:15
  30.2 7.2 %convert_reduce_fusion = (f32[256]{0:T(256)S(1)}, bf16[1,4096,256]{2,1,0:T(8,128)(2,1)S(1)}, bf16[1,4096,256]{2,1,0:T(8,128)(2,1)}) fusion(bf16[1,4096,256]{2,1,0:T(8,128)(2,1)S(1)} %copy-done.2, bf16[1,4096,256]{2,1,0:T(8,128)(2,1)S(1)} %get-tuple-element.21, f32[4096,256]{1,0:T(8,128)S(1)} %convolution_add_fusion.5, ...), kind=kOutput, calls=%fused_computation.47 | convolution fusion | flops 570425088 | bytes 15336448 | tf_op jit(solution)/shard_map/rtc,cd->rtd/dot_general | solution.py:26
  37.4 1.0 fusion.62
  39.7 2.1 collective-permute-start.2
  41.8 1.0 fusion.67
  42.8 1.0 fusion.70
  43.8 0.9 pad_maximum_fusion.2
  45.5 5.5 %collective-permute-done.2 = bf16[1,1024,256]{2,1,0:T(8,128)(2,1)S(1)} collective-permute-done((bf16[1,1024,256]{2,1,0:T(8,128)(2,1)S(1)}, bf16[1,1024,256]{2,1,0:T(8,128)(2,1)S(1)}, u32[]{:S(2)}, u32[]{:S(2)}) %collective-permute-start.2) | collective-permute-done | bytes 524320 | tf_op jit(solution)/shard_map/ppermute | solution.py:15
  51.0 6.9 %convert_reduce_fusion.1 = (f32[256]{0:T(256)S(1)}, bf16[1,4096,256]{2,1,0:T(8,128)(2,1)S(1)}, f32[1,4096,256]{2,1,0:T(8,128)}) fusion(f32[4096,256]{1,0:T(8,128)S(1)} %get-tuple-element.22, bf16[1,1024,256]{2,1,0:T(8,128)(2,1)S(1)} %collective-permute-done.2, bf16[1,4096,256]{2,1,0:T(8,128)(2,1)S(1)} %copy-done.2, ...), kind=kOutput, calls=%fused_computation.48 | convolution fusion | flops 565182208 | bytes 19530752 | tf_op jit(solution)/shard_map/rtd,cd->rtc/dot_general | solution.py:55
  57.9 1.0 fusion.78
  58.9 1.0 fusion.81
  61.8 1.9 collective-permute-start.3
  63.8 2.8 convolution_add_fusion.1
  67.5 85.0 %all-reduce.6 = (f32[256]{0:T(256)S(1)}, f32[256]{0:T(256)S(1)}) all-reduce(f32[256]{0:T(256)S(1)} %get-tuple-element.18, f32[256]{0:T(256)S(1)} %get-tuple-element.16), channel_id=1, replica_groups=mesh['frames'=32,'runs'=8] {'frames','runs'}, use_global_device_ids=true, to_apply=%region_2.3 | all-reduce | flops 512 | bytes 4096 | tf_op jit(solution)/shard_map/psum | solution.py:133
  153.0 8.1 %add_convert_fusion = bf16[1,4096,256]{2,1,0:T(8,128)(2,1)} fusion(f32[4096,256]{1,0:T(8,128)} %convolution_add_fusion.1, bf16[1,4096,256]{2,1,0:T(8,128)(2,1)S(1)} %get-tuple-element.19, bf16[1,512,256]{2,1,0:T(8,128)(2,1)S(1)} %collective-permute-done.3, f32[1,4096,256]{2,1,0:T(8,128)} %get-tuple-element.23, ...), kind=kOutput, calls=%fused_computation.49 | convolution fusion | flops 546308096 | bytes 15597568 | tf_op jit(solution)/shard_map/rtd,cd->rtc/dot_general | solution.py:55
  161.1 174.5 %all-reduce.10.cloned.1.call-done = (f32[3,256,256]{1,2,0:T(8,128)}, f32[3,256,256]{1,2,0:T(8,128)}) async-done(((f32[3,256,256]{1,2,0:T(8,128)}, f32[3,256,256]{1,2,0:T(8,128)}), (f32[3,256,256]{1,2,0:T(8,128)}, f32[3,256,256]{1,2,0:T(8,128)})) %all-reduce.10.cloned.1.call-update) | async-done | bytes 1572880 | tf_op jit(solution)/shard_map/psum | solution.py:133
  335.6 1.5 broadcast_multiply_fusion
  337.1 1.1 copy.18
  338.2 1.1 copy.17
  (32 shorter events, 9.5 us)
Async XLA Ops:
  7.2 328.4 %all-reduce.10.cloned.1.call-start = ((), (), s32[]{:S(2)}) async-start(), calls=%async_computation | async-start | bytes 3145728 | tf_op jit(solution)/shard_map/psum | solution.py:133
  8.2 7.8 %collective-permute-start = (bf16[1,512,256]{2,1,0:T(8,128)(2,1)S(1)}, bf16[1,512,256]{2,1,0:T(8,128)(2,1)S(1)}, u32[]{:S(2)}, u32[]{:S(2)}) collective-permute-start(bf16[1,512,256]{2,1,0:T(8,128)(2,1)S(1)} %slice.77), channel_id=1, source_target_pairs={{0,8},{8,16},{16,24},{24,32},{32,40},{40,48},{48,56},{56,64},{64,7... | collective-permute-start | bytes 786440 | tf_op jit(solution)/shard_map/ppermute | solution.py:15
  13.4 2.7 copy-start
  15.8 1.0 copy-start.1
  17.5 5.8 %copy-start.4 = (bf16[256]{0:T(256)(128)(2,1)S(1)}, bf16[256]{0:T(256)(128)(2,1)}, u32[]{:S(2)}) copy-start(bf16[256]{0:T(256)(128)(2,1)} %param.10) | copy-start | bytes 1540
  17.6 5.8 %copy-start.3 = (bf16[3,256,256]{2,1,0:T(8,128)(2,1)S(1)}, bf16[3,256,256]{2,1,0:T(8,128)(2,1)}, u32[]{:S(2)}) copy-start(bf16[3,256,256]{2,1,0:T(8,128)(2,1)} %param.9) | copy-start | bytes 1179652
  19.5 9.9 %collective-permute-start.1 = (bf16[1,1024,256]{2,1,0:T(8,128)(2,1)S(1)}, bf16[1,1024,256]{2,1,0:T(8,128)(2,1)S(1)}, u32[]{:S(2)}, u32[]{:S(2)}) collective-permute-start(bf16[1,1024,256]{2,1,0:T(8,128)(2,1)S(1)} %slice.98), channel_id=1, source_target_pairs={{0,8},{8,16},{16,24},{24,32},{32,40},{40,48},{48,56},{56,64},{64,7... | collective-permute-start | bytes 1572872 | tf_op jit(solution)/shard_map/ppermute | solution.py:15
  24.0 6.1 %copy-start.2 = (bf16[1,4096,256]{2,1,0:T(8,128)(2,1)S(1)}, bf16[1,4096,256]{2,1,0:T(8,128)(2,1)}, u32[]{:S(2)}) copy-start(bf16[1,4096,256]{2,1,0:T(8,128)(2,1)} %param.11) | copy-start | bytes 6291460
  39.7 11.2 %collective-permute-start.2 = (bf16[1,1024,256]{2,1,0:T(8,128)(2,1)S(1)}, bf16[1,1024,256]{2,1,0:T(8,128)(2,1)S(1)}, u32[]{:S(2)}, u32[]{:S(2)}) collective-permute-start(bf16[1,1024,256]{2,1,0:T(8,128)(2,1)S(1)} %fusion.59), channel_id=1, source_target_pairs={{8,0},{16,8},{24,16},{32,24},{40,32},{48,40},{56,48},{64,56},{72,6... | collective-permute-start | bytes 1572872 | tf_op jit(solution)/shard_map/ppermute | solution.py:15
  61.8 91.2 %collective-permute-start.3 = (bf16[1,512,256]{2,1,0:T(8,128)(2,1)S(1)}, bf16[1,512,256]{2,1,0:T(8,128)(2,1)S(1)}, u32[]{:S(2)}, u32[]{:S(2)}) collective-permute-start(bf16[1,512,256]{2,1,0:T(8,128)(2,1)S(1)} %fusion.61), channel_id=1, source_target_pairs={{8,0},{16,8},{24,16},{32,24},{40,32},{48,40},{56,48},{64,56},{72,6... | collective-permute-start | bytes 786440 | tf_op jit(solution)/shard_map/ppermute | solution.py:15
Sparse Core Ops, SparseCore 0:
  67.6 267.9 all-reduce.9
where the time goes:
time: 347 us; the launch traced here: 346 us
  waiting for transfers between devices  186 us (54%)
  blocking collectives  85 us (24%)
  matrix products  40.4 us (12%)
  between operations  14.3 us (4%)
  starting transfers between devices  12.3 us (4%)
  other arithmetic  4.58 us (1%)
  local copies, waits for them, and re-layouts  4.12 us (1%)
    psum x1, waiting for transfers between devices, body(): lax.psum((first_weight_delta, db_first, second_weight_delta, db_second),...  174 us
    psum x1, blocking collectives, body(): lax.psum((first_weight_delta, db_first, second_weight_delta, db_second),...  85 us
    dot_general x6, matrix products, local_terms(): jnp.einsum('rtd,cd->rtc', padded[:, start:start + frame_count], weights[k...  20 us
    dot_general x6, matrix products, causal_conv_apply(): jnp.einsum('rtc,cd->rtd', extended[:, start:start + frame_count], weights...  13.8 us
    ppermute x4, starting transfers between devices, passed_along(): return lax.ppermute(block, axis, route)  12.3 us
    ppermute x4, waiting for transfers between devices, passed_along(): return lax.ppermute(block, axis, route)  11 us
  transfers between devices with their start and end apart: 5, of which 4 were waited for; matrix products, arithmetic and copies ran while one was open for 6% of the time, Pallas kernels for 0%

commit v1 on v0

v1 whole, which is shorter than its diff:
```python
import functools
import math

import jax
import jax.numpy as jnp
from jax import lax
from jax.experimental import pallas as pl
from jax.experimental.pallas import tpu as pltpu
from jax.sharding import PartitionSpec as P

C = 256
D1 = 256
D2 = 512
H1 = 2 * D1
H2 = 2 * D2
R = 512
F32 = jnp.float32
BF16 = jnp.bfloat16
C0 = math.sqrt(2.0 / math.pi)
C1 = C0 * 0.044715
MESH = pl.DeviceIdType.MESH


def gelu_parts(v):
    v2 = v * v
    t = jnp.tanh(v * (C0 + C1 * v2))
    h = 0.5 * v
    act = h + h * t
    slope = (0.5 + 0.5 * t) + (h * (1.0 - t * t)) * (C0 + (3.0 * C1) * v2)
    return act, slope


def dot(a, b):
    return jnp.dot(a, b, preferred_element_type=F32)


class Place:
    sizes = {"core": 2, "x": 4, "y": 4, "z": 8}

    def __init__(self):
        self.f = lax.axis_index("frames")
        self.r = lax.axis_index("runs")
        self.core = lax.rem(self.f, 2)
        self.xl = lax.rem(self.f // 2, 2)
        self.z = self.f // 4
        self.xh = lax.rem(self.r, 2)
        self.y = self.r // 2
        self.x = self.xh * 2 + self.xl

    def index(self, axis):
        return {"core": self.core, "x": self.x, "y": self.y, "z": self.z}[axis]

    def other(self, axis, d):
        return lax.rem(self.index(axis) + d, self.sizes[axis])

    def peer(self, axis, i):
        if axis == "core":
            return (self.f - self.core + i, self.r)
        if axis == "x":
            return (self.z * 4 + lax.rem(i, 2) * 2 + self.core, self.y * 2 + i // 2)
        if axis == "y":
            return (self.f, i * 2 + self.xh)
        return (i * 4 + self.xl * 2 + self.core, self.r)


class Part:
    def __init__(self, place, order, refs, send, recv):
        self.p = place
        self.a, self.b = order
        self.s0, self.r0, self.s1, self.r1, self.s2, self.r2, self.zb, self.fin = refs
        self.send, self.recv = send, recv
        self.sem = 0
        self.open = []

    def put(self, src, dst, to):
        copy = pltpu.make_async_remote_copy(
            src_ref=src,
            dst_ref=dst,
            send_sem=self.send.at[self.sem],
            recv_sem=self.recv.at[self.sem],
            device_id=to,
            device_id_type=MESH,
        )
        self.sem += 1
        copy.start()
        self.open.append(copy)

    def drain(self):
        for copy in self.open:
            copy.wait()
        self.open = []

    def steps(self):
        return [self.step0, self.step1, self.step2, self.step3, self.step4, self.step5, self.step6, self.drain]

    def step0(self):
        o = self.p.other("core", 1)
        self.put(self.s0.at[o], self.r0, self.p.peer("core", o))

    def step1(self):
        self.drain()
        c = self.p.core
        self.s1[...] = (self.s0[c].astype(F32) + self.r0[...].astype(F32)).astype(BF16)
        for d in range(1, 4):
            o = self.p.other(self.a, d)
            self.put(self.s1.at[o], self.r1.at[d - 1], self.p.peer(self.a, o))

    def step2(self):
        self.drain()
        i = self.p.index(self.a)
        total = self.s1[i].astype(F32)
        for d in range(3):
            total = total + self.r1[d].astype(F32)
        self.s2[...] = total.astype(BF16)
        for d in range(1, 4):
            o = self.p.other(self.b, d)
            self.put(self.s2.at[o // 2, lax.rem(o, 2)], self.r2.at[d - 1], self.p.peer(self.b, o))

    def step3(self):
        self.drain()
        i = self.p.index(self.b)
        total = self.s2[i // 2, lax.rem(i, 2)].astype(F32)
        for d in range(3):
            total = total + self.r2[d].astype(F32)
        z = self.p.z
        self.zb[z] = total.astype(BF16)
        for d in range(1, 8):
            o = self.p.other("z", d)
            self.put(self.zb.at[z], self.zb.at[z], self.p.peer("z", o))

    def step4(self):
        self.drain()
        total = self.zb[0].astype(F32)
        for i in range(1, 8):
            total = total + self.zb[i].astype(F32)
        c, i, j = self.p.core, self.p.index(self.a), self.p.index(self.b)
        mine = self.fin.at[c, i, j // 2, lax.rem(j, 2)]
        mine[...] = total.astype(BF16)
        for d in range(1, 4):
            o = self.p.other(self.b, d)
            self.put(mine, mine, self.p.peer(self.b, o))

    def step5(self):
        self.drain()
        mine = self.fin.at[self.p.core, self.p.index(self.a)]
        for d in range(1, 4):
            o = self.p.other(self.a, d)
            self.put(mine, mine, self.p.peer(self.a, o))

    def step6(self):
        self.drain()
        mine = self.fin.at[self.p.core]
        self.put(mine, mine, self.p.peer("core", self.p.other("core", 1)))


PART_SHAPES = [
    (2, 4, 2, 2, 24, 128),
    (4, 2, 2, 24, 128),
    (4, 2, 2, 24, 128),
    (3, 2, 2, 24, 128),
    (2, 2, 24, 128),
    (3, 24, 128),
    (8, 24, 128),
    (2, 4, 2, 2, 24, 128),
]
PART_SEMS = 21


class BiasSum:
    axes = ("core", "x", "y", "z")

    def __init__(self, place, slots, send, recv):
        self.p, self.slots, self.send, self.recv = place, slots, send, recv
        self.sem = 0
        self.open = []

    def exchange(self, axis, buf):
        i = self.p.index(axis)
        for d in range(1, self.p.sizes[axis]):
            copy = pltpu.make_async_remote_copy(
                src_ref=buf.at[i],
                dst_ref=buf.at[i],
                send_sem=self.send.at[self.sem],
                recv_sem=self.recv.at[self.sem],
                device_id=self.p.peer(axis, self.p.other(axis, d)),
                device_id_type=MESH,
            )
            self.sem += 1
            copy.start()
            self.open.append(copy)

    def begin(self, level, value):
        axis, buf = self.axes[level], self.slots[level]
        buf[self.p.index(axis)] = value
        self.exchange(axis, buf)

    def finish(self, level):
        for copy in self.open:
            copy.wait()
        self.open = []
        buf = self.slots[level]
        total = buf[0]
        for i in range(1, self.p.sizes[self.axes[level]]):
            total = total + buf[i]
        return total


def kernel(
    frames,
    x_hbm, up_hbm, w1, b1, w2, b2,
    out_hbm, gin_hbm, gw1, gb1, gw2, gb2,
    xin, up, hid, xt, hidt, s1, g2, gh, g1, outb, ginb, w1t, w2t, acc1, acc2, db1, db2,
    *rest,
):
    nb = frames // R
    bufs, rest = rest[: 4 * len(PART_SHAPES)], rest[4 * len(PART_SHAPES) :]
    slots, rest = rest[:4], rest[4:]
    load_sem, out_sem, halo_send, halo_recv, ar_send, ar_recv, bias_send, bias_recv = rest

    place = Place()
    f, r = place.f, place.r
    n = lax.axis_size("frames")
    after = (lax.rem(f + 1, n), r)
    before = (lax.rem(f + n - 1, n), r)

    barrier = pltpu.get_barrier_semaphore()
    peers = [after, before]
    for axis, size in Place.sizes.items():
        for d in range(1, size):
            peers.append(place.peer(axis, place.other(axis, d)))
    for peer in peers:
        pl.semaphore_signal(barrier, inc=1, device_id=peer, device_id_type=MESH)

    tail = 3 * R
    loads = [
        pltpu.make_async_copy(x_hbm.at[pl.ds(frames - tail, tail)], xin.at[pl.ds(H1 + frames - tail, tail)], load_sem.at[0]),
        pltpu.make_async_copy(x_hbm.at[pl.ds(0, frames - tail)], xin.at[pl.ds(H1, frames - tail)], load_sem.at[1]),
        pltpu.make_async_copy(up_hbm, up, load_sem.at[2]),
    ]
    for copy in loads:
        copy.start()

    def halo(k, src, dst, to):
        return pltpu.make_async_remote_copy(
            src_ref=src, dst_ref=dst, send_sem=halo_send.at[k], recv_sem=halo_recv.at[k],
            device_id=to, device_id_type=MESH,
        )

    send_x = halo(0, xin.at[pl.ds(frames, H1)], xin.at[pl.ds(0, H1)], after)
    send_h = halo(1, hid.at[pl.ds(frames, H2)], hid.at[pl.ds(0, H2)], after)
    send_g2 = halo(2, g2.at[pl.ds(0, H2)], g2.at[pl.ds(frames, H2)], before)
    send_g1 = halo(3, g1.at[pl.ds(0, H1)], g1.at[pl.ds(frames, H1)], before)

    for k in range(3):
        w1t[pl.ds(k * C, C), :] = w1[pl.ds(k * C, C), :].T
        w2t[pl.ds(k * C, C), :] = w2[pl.ds(k * C, C), :].T
    acc1[...] = jnp.zeros_like(acc1)
    acc2[...] = jnp.zeros_like(acc2)
    db1[...] = jnp.zeros_like(db1)
    db2[...] = jnp.zeros_like(db2)
    bias1 = b1[...].astype(F32)
    bias2 = b2[...].astype(F32)

    def rows(start, size=R):
        return pl.ds(pl.multiple_of(start, 256), size)

    def block_f1(b):
        t = b * R
        x0 = xin[rows(t + H1), :]
        x1 = xin[rows(t + H1 - D1), :]
        x2 = xin[rows(t), :]
        pre = dot(jnp.concatenate([x0, x1, x2], axis=1), w1[...]) + bias1
        act, slope = gelu_parts(pre)
        h = (x0.astype(F32) + act).astype(BF16)
        hid[rows(t + H2), :] = h
        s1[rows(t), :] = slope
        xt[:, rows(t + H1)] = x0.T
        hidt[:, rows(t + H2)] = h.T

    def block_f2(b):
        t = b * R
        h0 = hid[rows(t + H2), :]
        h1 = hid[rows(t + H2 - D2), :]
        h2 = hid[rows(t), :]
        pre = dot(jnp.concatenate([h0, h1, h2], axis=1), w2[...]) + bias2
        act, slope = gelu_parts(pre)
        outb[rows(t), :] = (h0.astype(F32) + act).astype(BF16)
        g = up[rows(t), :].astype(F32) * slope
        db2[...] += jnp.sum(g.reshape(R // 8, 8, C), axis=0)
        gb = g.astype(BF16)
        g2[rows(t), :] = gb
        for k in range(3):
            acc2[pl.ds(k * C, C), :] += dot(hidt[:, rows(t + H2 - k * D2)], gb)
        out_copy(b).start()

    def block_b2(b):
        t = b * R
        cat = jnp.concatenate([g2[rows(t + k * D2), :] for k in range(3)], axis=1)
        grad = dot(cat, w2t[...]) + up[rows(t), :].astype(F32)
        gh[rows(t), :] = grad
        g = grad * s1[rows(t), :]
        db1[...] += jnp.sum(g.reshape(R // 8, 8, C), axis=0)
        gb = g.astype(BF16)
        g1[rows(t), :] = gb
        for k in range(3):
            acc1[pl.ds(k * C, C), :] += dot(xt[:, rows(t + H1 - k * D1)], gb)

    def block_b1(b):
        t = b * R
        cat = jnp.concatenate([g1[rows(t + k * D1), :] for k in range(3)], axis=1)
        ginb[rows(t), :] = (dot(cat, w1t[...]) + gh[rows(t), :]).astype(BF16)
        gin_copy(b).start()

    def out_copy(b):
        return pltpu.make_async_copy(outb.at[rows(b * R)], out_hbm.at[rows(b * R)], out_sem.at[b])

    def gin_copy(b):
        return pltpu.make_async_copy(ginb.at[rows(b * R)], gin_hbm.at[rows(b * R)], out_sem.at[nb + b])

    def loop(lo, hi, block):
        if hi - lo == 1:
            block(lo)
            return

        def body(b, _):
            block(b)
            return 0

        lax.fori_loop(lo, hi, body, 0)

    def parts_of(layer):
        made = []
        for q, order in enumerate((("x", "y"), ("y", "x"))):
            k = layer * 2 + q
            refs = bufs[k * len(PART_SHAPES) : (k + 1) * len(PART_SHAPES)]
            made.append(Part(place, order, refs, ar_send.at[k], ar_recv.at[k]))
        return made

    def pack(acc, made):
        for q, part in enumerate(made):
            for h in range(2):
                piece = acc[pl.ds(q * 384, 384), pl.ds(h * 128, 128)] * (1.0 / 1024.0)
                part.s0[:, :, :, h] = piece.reshape(2, 4, 2, 24, 128).astype(BF16)

    def unpack(acc, made):
        for q, part in enumerate(made):
            for h in range(2):
                acc[pl.ds(q * 384, 384), pl.ds(h * 128, 128)] = (
                    part.fin[:, :, :, h].astype(F32).reshape(384, 128)
                )

    def run(made, k):
        for part in made:
            part.steps()[k]()

    loads[0].wait()
    loop(nb - 2, nb, block_f1)
    pl.semaphore_wait(barrier, len(peers))
    send_x.start()
    send_h.start()
    loads[1].wait()
    loop(1, nb - 2, block_f1)
    send_x.wait()

    @pl.when(f == 0)
    def _():
        xin[pl.ds(0, H1), :] = jnp.zeros((H1, C), BF16)

    xt[:, pl.ds(0, H1)] = xin[pl.ds(0, H1), :].T
    loop(0, 1, block_f1)
    send_h.wait()

    @pl.when(f == 0)
    def _():
        hid[pl.ds(0, H2), :] = jnp.zeros((H2, C), BF16)

    hidt[:, pl.ds(0, H2)] = hid[pl.ds(0, H2), :].T

    loads[2].wait()
    loop(0, 2, block_f2)
    send_g2.start()
    loop(2, nb, block_f2)
    layer2 = parts_of(1)
    pack(acc2, layer2)
    run(layer2, 0)

    loop(0, 1, block_b2)
    send_g1.start()
    run(layer2, 1)
    loop(1, 3, block_b2)
    run(layer2, 2)
    loop(3, nb - 2, block_b2)
    run(layer2, 3)
    send_g2.wait()

    @pl.when(f == n - 1)
    def _():
        g2[pl.ds(frames, H2), :] = jnp.zeros((H2, C), BF16)

    loop(nb - 2, nb, block_b2)
    layer1 = parts_of(0)
    pack(acc1, layer1)
    run(layer1, 0)
    bias = BiasSum(place, slots, bias_send, bias_recv)
    both = jnp.concatenate(
        [jnp.sum(v[...], axis=0, keepdims=True)[:, h * 128 : (h + 1) * 128] for v in (db2, db1) for h in range(2)]
        + [jnp.zeros((4, 128), F32)],
        axis=0,
    ) * (1.0 / 1024.0)
    bias.begin(0, both)
    run(layer2, 4)
    loop(0, 2, block_b1)
    run(layer1, 1)
    bias.begin(1, bias.finish(0))
    run(layer2, 5)
    loop(2, 5, block_b1)
    run(layer1, 2)
    bias.begin(2, bias.finish(1))
    run(layer2, 6)
    loop(5, nb - 1, block_b1)
    send_g1.wait()

    @pl.when(f == n - 1)
    def _():
        g1[pl.ds(frames, H1), :] = jnp.zeros((H1, C), BF16)

    loop(nb - 1, nb, block_b1)
    run(layer1, 3)
    bias.begin(3, bias.finish(2))
    run(layer2, 7)
    unpack(gw2, layer2)
    run(layer1, 4)
    total = bias.finish(3)
    for h in range(2):
        gb2[:, pl.ds(h * 128, 128)] = total[h : h + 1]
        gb1[:, pl.ds(h * 128, 128)] = total[2 + h : 3 + h]
    run(layer1, 5)
    run(layer1, 6)
    for b in range(nb):
        out_copy(b).wait()
        gin_copy(b).wait()
    run(layer1, 7)
    unpack(gw1, layer1)


def body(inputs, first_layer_weight, first_layer_bias, second_layer_weight, second_layer_bias, upstream):
    _, frames, c = inputs.shape
    any_spec = pl.BlockSpec(memory_space=pl.ANY)
    vmem = pl.BlockSpec(memory_space=pltpu.VMEM)
    nb = frames // R
    scratch = [
        pltpu.VMEM((H1 + frames, C), BF16),
        pltpu.VMEM((frames, C), BF16),
        pltpu.VMEM((H2 + frames, C), BF16),
        pltpu.VMEM((C, H1 + frames), BF16),
        pltpu.VMEM((C, H2 + frames), BF16),
        pltpu.VMEM((frames, C), F32),
        pltpu.VMEM((frames + H2, C), BF16),
        pltpu.VMEM((frames, C), F32),
        pltpu.VMEM((frames + H1, C), BF16),
        pltpu.VMEM((frames, C), BF16),
        pltpu.VMEM((frames, C), BF16),
        pltpu.VMEM((3 * C, C), BF16),
        pltpu.VMEM((3 * C, C), BF16),
        pltpu.VMEM((3 * C, C), F32),
        pltpu.VMEM((3 * C, C), F32),
        pltpu.VMEM((8, C), F32),
        pltpu.VMEM((8, C), F32),
    ]
    scratch += [pltpu.VMEM(shape, BF16) for _ in range(4) for shape in PART_SHAPES]
    scratch += [pltpu.VMEM((k, 8, 128), F32) for k in (2, 4, 4, 8)]
    scratch += [
        pltpu.SemaphoreType.DMA((3,)),
        pltpu.SemaphoreType.DMA((2 * nb,)),
        pltpu.SemaphoreType.DMA((4,)),
        pltpu.SemaphoreType.DMA((4,)),
        pltpu.SemaphoreType.DMA((4, PART_SEMS)),
        pltpu.SemaphoreType.DMA((4, PART_SEMS)),
        pltpu.SemaphoreType.DMA((14,)),
        pltpu.SemaphoreType.DMA((14,)),
    ]
    outs = pl.pallas_call(
        functools.partial(kernel, frames),
        out_shape=[
            jax.ShapeDtypeStruct((frames, c), BF16),
            jax.ShapeDtypeStruct((frames, c), BF16),
            jax.ShapeDtypeStruct((3 * C, C), F32),
            jax.ShapeDtypeStruct((1, C), F32),
            jax.ShapeDtypeStruct((3 * C, C), F32),
            jax.ShapeDtypeStruct((1, C), F32),
        ],
        in_specs=[any_spec, any_spec, vmem, vmem, vmem, vmem],
        out_specs=[any_spec, any_spec, vmem, vmem, vmem, vmem],
        scratch_shapes=scratch,
        compiler_params=pltpu.CompilerParams(
            collective_id=0, has_side_effects=True, vmem_limit_bytes=56 * 1024 * 1024
        ),
    )(
        inputs.reshape(frames, c),
        upstream.reshape(frames, c),
        first_layer_weight.reshape(3 * C, C),
        first_layer_bias.reshape(1, C),
        second_layer_weight.reshape(3 * C, C),
        second_layer_bias.reshape(1, C),
    )
    out, gin, gw1, gb1, gw2, gb2 = outs
    return (
        out.reshape(1, frames, c),
        gin.reshape(1, frames, c),
        gw1.reshape(3, C, C),
        gb1.reshape(C),
        gw2.reshape(3, C, C),
        gb2.reshape(C),
    )


def solution(mesh):
    return jax.shard_map(
        body,
        mesh=mesh,
        in_specs=(P("runs", "frames", None), P(), P(), P(), P(), P("runs", "frames", None)),
        out_specs=(P("runs", "frames", None), P("runs", "frames", None), P(), P(), P(), P()),
        check_vma=False,
    )
```

time: 347 us -> 86.7 us (0.25)
  waiting for transfers between devices: 186 us -> 0 us
  blocking collectives: 85 us -> 0 us
  Pallas kernels: 0 us -> 75.7 us
  matrix products: 40.4 us -> 0 us
  between operations: 14.3 us -> 0.66 us
  starting transfers between devices: 12.3 us -> 0 us
  local copies, waits for them, and re-layouts: 4.12 us -> 10.2 us
  other arithmetic: 4.58 us -> 0 us
    psum x1 -> x0, waiting for transfers between devices: 174 us -> none  [body(): lax.psum((first_weight_delta, db_first, second_weight_delta, db_second),...]
    psum x1 -> x0, blocking collectives: 85 us -> none  [body(): lax.psum((first_weight_delta, db_first, second_weight_delta, db_second),...]
    pallas_call x0 -> x1, Pallas kernels: none -> 75.7 us  [body(): pl.pallas_call(functools.partial(kernel, frames), out_shape=[jax.ShapeDty...]
    dot_general x22 -> x0, matrix products: 40.4 us -> none  [the longest x6 20 us: local_terms(): jnp.einsum('rtd,cd->rtc', padded[:, start:start + frame_count], weights[k...]
    ppermute x4 -> x0, starting transfers between devices: 12.3 us -> none  [passed_along(): return lax.ppermute(block, axis, route)]
    ppermute x4 -> x0, waiting for transfers between devices: 11 us -> none  [passed_along(): return lax.ppermute(block, axis, route)]
    unnamed x13 -> x16, local copies, waits for them, and re-layouts: 2.98 us -> 7.74 us
  transfers between devices with their start and end apart: 5 -> 0, of which waited for: 4 -> 0; matrix products, arithmetic and copies ran while one was open for 6% -> 0% of each run, Pallas kernels for 0% -> 0%
where the time goes in v1:
time: 86.7 us; the launch traced here: 86.5 us
  Pallas kernels  75.7 us (87%)
  local copies, waits for them, and re-layouts  10.2 us (12%)
    pallas_call x1, Pallas kernels, body(): pl.pallas_call(functools.partial(kernel, frames), out_shape=[jax.ShapeDty...  75.7 us
    unnamed x16, local copies, waits for them, and re-layouts  7.74 us

profile of v1, /device:TPU:1, one launch (start us, length us, event | category | flops | bytes accessed | tf_op | source)
XLA Modules:
  0.0 86.5 jit_solution(17505927914893441713)
XLA Ops:
  0.6 1.2 %reshape.51.b1 = bf16[1,256]{1,0:T(2,128)(2,1)} reshape(bf16[256]{0:T(256)(128)(2,1)} %param.8) | data formatting | bytes 1024 | tf_op jit(solution)/shard_map/reshape | solution.py:502
  1.9 1.2 %reshape.53.b2 = bf16[1,256]{1,0:T(2,128)(2,1)} reshape(bf16[256]{0:T(256)(128)(2,1)} %param.10) | data formatting | bytes 1024 | tf_op jit(solution)/shard_map/reshape | solution.py:504
  3.1 75.7 %shard_map.109 = (bf16[4096,256]{1,0:T(8,128)(2,1)}, bf16[4096,256]{1,0:T(8,128)(2,1)}, f32[768,256]{1,0:T(8,128)}, f32[1,256]{1,0:T(1,128)}, f32[768,256]{1,0:T(8,128)}, /*index=5*/f32[1,256]{1,0:T(1,128)}) custom-call(bf16[4096,256]{1,0:T(8,128)(2,1)} %bitcast.10, bf16[4096,256]{1,0:T(8,128)(2,1)} %bitcast.11, bf16[768,256]{1,0:T(8,128)(2,1)} %bitcast.16, ...), custom_call_target="tpu_custom_call" | custom-call | tf_op jit(solution)/shard_map/pallas_call | solution.py:482
  78.8 0.0 copy-start
  78.8 3.2 %copy.18 = bf16[1,4096,256]{2,1,0:T(8,128)(2,1)} copy(bf16[1,4096,256]{2,1,0:T(8,128)(2,1)} %bitcast.13) | data formatting | bytes 4194304
  82.0 0.0 copy-done
  82.0 0.0 copy-start.2
  82.0 0.0 copy-start.4
  82.0 0.0 copy-start.1
  82.0 1.3 %copy.19 = bf16[1,4096,256]{2,1,0:T(8,128)(2,1)} copy(bf16[1,4096,256]{2,1,0:T(8,128)(2,1)S(1)} %bitcast.12) | data formatting | bytes 4194304
  83.3 0.3 copy-done.2
  83.6 0.0 copy-start.3
  83.6 0.9 %copy.20 = f32[3,256,256]{2,1,0:T(8,128)} copy(f32[3,256,256]{2,1,0:T(8,128)S(1)} %bitcast.15) | data formatting | bytes 1572864
  84.5 0.0 copy-done.4
  84.5 0.6 copy.21
  85.1 0.0 copy-done.1
  85.1 0.9 %copy.22 = f32[3,256,256]{2,1,0:T(8,128)} copy(f32[3,256,256]{2,1,0:T(8,128)S(1)} %bitcast.14) | data formatting | bytes 1572864
  86.0 0.0 copy-done.3
  86.0 0.6 copy.23
Async XLA Ops:
  78.8 3.2 %copy-start = (bf16[4096,256]{1,0:T(8,128)(2,1)S(1)}, bf16[4096,256]{1,0:T(8,128)(2,1)}, u32[]{:S(2)}) copy-start(bf16[4096,256]{1,0:T(8,128)(2,1)} %get-tuple-element.13) | copy-start | bytes 6291460
  82.0 1.7 %copy-start.2 = (f32[768,256]{1,0:T(8,128)S(1)}, f32[768,256]{1,0:T(8,128)}, u32[]{:S(2)}) copy-start(f32[768,256]{1,0:T(8,128)} %get-tuple-element.14) | copy-start | bytes 2359300
  82.0 2.5 %copy-start.4 = (f32[1,256]{1,0:T(1,128)S(1)}, f32[1,256]{1,0:T(1,128)}, u32[]{:S(2)}) copy-start(f32[1,256]{1,0:T(1,128)} %get-tuple-element.15) | copy-start | bytes 3076
  82.0 3.1 %copy-start.1 = (f32[768,256]{1,0:T(8,128)S(1)}, f32[768,256]{1,0:T(8,128)}, u32[]{:S(2)}) copy-start(f32[768,256]{1,0:T(8,128)} %get-tuple-element.16) | copy-start | bytes 2359300
  83.6 2.3 %copy-start.3 = (f32[1,256]{1,0:T(1,128)S(1)}, f32[1,256]{1,0:T(1,128)}, u32[]{:S(2)}) copy-start(f32[1,256]{1,0:T(1,128)} %get-tuple-element.17) | copy-start | bytes 3076

commit v2 on v1

v2 whole, which is shorter than its diff:
```python
import functools
import itertools
import math

import jax
import jax.numpy as jnp
from jax import lax
from jax.experimental import pallas as pl
from jax.experimental.pallas import tpu as pltpu
from jax.sharding import PartitionSpec as P

C = 256
D1 = 256
D2 = 512
HX = 1536
HH = 1024
R = 512
F32 = jnp.float32
BF16 = jnp.bfloat16
C0 = math.sqrt(2.0 / math.pi)
C1 = C0 * 0.044715
MESH = pl.DeviceIdType.MESH


def gelu_parts(v):
    v2 = v * v
    t = jnp.tanh(v * (C0 + C1 * v2))
    h = 0.5 * v
    act = h + h * t
    slope = (0.5 + 0.5 * t) + (h * (1.0 - t * t)) * (C0 + (3.0 * C1) * v2)
    return act, slope


def dot(a, b):
    return jnp.dot(a, b, preferred_element_type=F32)


def dot_rows(a, b):
    return lax.dot_general(a, b, (((0,), (0,)), ((), ())), preferred_element_type=F32)


class Place:
    sizes = {"core": 2, "xy": 16, "z": 8}

    def __init__(self):
        self.f = lax.axis_index("frames")
        self.r = lax.axis_index("runs")
        self.core = lax.rem(self.f, 2)
        self.z = self.f // 4
        self.x = lax.rem(self.r, 2) * 2 + lax.rem(self.f // 2, 2)
        self.y = self.r // 2

    def device(self, core, x, y, z):
        return (z * 4 + lax.rem(x, 2) * 2 + core, y * 2 + x // 2)

    def index(self, group):
        return {"core": self.core, "xy": self.x * 4 + self.y, "z": self.z}[group]

    def others(self, group):
        if group == "core":
            o = 1 - self.core
            return [(o, self.device(o, self.x, self.y, self.z))]
        if group == "z":
            found = []
            for d in (4, 3, 5, 2, 6, 1, 7):
                o = lax.rem(self.z + d, 8)
                found.append((o, self.device(self.core, self.x, self.y, o)))
            return found
        steps = [s for s in itertools.product(range(4), range(4)) if any(s)]
        steps.sort(key=lambda s: -sum(min(v, 4 - v) for v in s))
        found = []
        for dx, dy in steps:
            x, y = lax.rem(self.x + dx, 4), lax.rem(self.y + dy, 4)
            found.append((x * 4 + y, self.device(self.core, x, y, self.z)))
        return found


class Sender:
    def __init__(self, place, send, recv):
        self.p, self.send, self.recv = place, send, recv
        self.sem = 0
        self.open = []

    def put(self, src, dst, to):
        copy = pltpu.make_async_remote_copy(
            src_ref=src,
            dst_ref=dst,
            send_sem=self.send.at[self.sem],
            recv_sem=self.recv.at[self.sem],
            device_id=to,
            device_id_type=MESH,
        )
        self.sem += 1
        copy.start()
        self.open.append(copy)

    def drain(self):
        for copy in self.open:
            copy.wait()
        self.open = []


class Part(Sender):
    sems = 1 + 15 + 7 + 15 + 1

    def __init__(self, place, a, b, refs, send, recv):
        super().__init__(place, send, recv)
        self.a, self.b = a, b
        self.s0, self.r0, self.s1, self.r1, self.zb, self.fin = refs

    @staticmethod
    def shapes(a, b):
        n2 = Place.sizes[b]
        inner = (8, 2, 24, 128) if a == "xy" else (8, 24, 256)
        chunk = inner[-2:]
        n1 = Place.sizes[a]
        return [(2,) + inner, inner, inner, (n1 - 1,) + chunk, (n2,) + chunk, (2,) + inner]

    def chunk(self, ref, lead, j):
        where = (j // 2, lax.rem(j, 2)) if self.a == "xy" else (j,)
        return ref.at[lead + where]

    def step0(self):
        for o, to in self.p.others("core"):
            self.put(self.s0.at[o], self.r0, to)

    def step1(self):
        self.drain()
        self.s1[...] = (self.s0[self.p.core].astype(F32) + self.r0[...].astype(F32)).astype(BF16)
        for d, (o, to) in enumerate(self.p.others(self.a)):
            self.put(self.chunk(self.s1, (), o), self.r1.at[d], to)

    def step2(self):
        self.drain()
        total = self.chunk(self.s1, (), self.p.index(self.a))[...].astype(F32)
        for d in range(Place.sizes[self.a] - 1):
            total = total + self.r1[d].astype(F32)
        i = self.p.index(self.b)
        self.zb[i] = total.astype(BF16)
        for o, to in self.p.others(self.b):
            self.put(self.zb.at[i], self.zb.at[i], to)

    def step3(self):
        self.drain()
        total = self.zb[0].astype(F32)
        for i in range(1, Place.sizes[self.b]):
            total = total + self.zb[i].astype(F32)
        mine = self.chunk(self.fin, (self.p.core,), self.p.index(self.a))
        mine[...] = total.astype(BF16)
        for o, to in self.p.others(self.a):
            self.put(mine, mine, to)

    def step4(self):
        self.drain()
        mine = self.fin.at[self.p.core]
        for o, to in self.p.others("core"):
            self.put(mine, mine, to)

    def pack(self, acc, row):
        if self.a == "xy":
            for h in range(2):
                piece = acc[pl.ds(row, 384), pl.ds(h * 128, 128)] * (1.0 / 1024.0)
                self.s0[:, :, h] = piece.reshape(2, 8, 24, 128).astype(BF16)
        else:
            piece = acc[pl.ds(row, 384), :] * (1.0 / 1024.0)
            self.s0[...] = piece.reshape(2, 8, 24, 256).astype(BF16)

    def unpack(self, out, row):
        if self.a == "xy":
            for h in range(2):
                out[pl.ds(row, 384), pl.ds(h * 128, 128)] = self.fin[:, :, h].astype(F32).reshape(384, 128)
        else:
            out[pl.ds(row, 384), :] = self.fin[...].astype(F32).reshape(384, 256)


class Layer:
    groups = (("xy", "z"), ("z", "xy"))

    def __init__(self, place, refs, send, recv):
        self.parts = []
        for q, (a, b) in enumerate(self.groups):
            self.parts.append(Part(place, a, b, refs[q * 6 : q * 6 + 6], send.at[q], recv.at[q]))

    def begin(self, acc):
        for q, part in enumerate(self.parts):
            part.pack(acc, q * 384)
            part.step0()

    def step(self, k):
        for part in self.parts:
            getattr(part, "step%d" % k)()

    def end(self, out):
        for q, part in enumerate(self.parts):
            part.drain()
            part.unpack(out, q * 384)


class BiasSum(Sender):
    groups = ("core", "xy", "z")

    def __init__(self, place, slots, send, recv):
        super().__init__(place, send, recv)
        self.slots = slots

    def begin(self, level, value):
        group, buf = self.groups[level], self.slots[level]
        i = self.p.index(group)
        buf[i] = value
        for o, to in self.p.others(group):
            self.put(buf.at[i], buf.at[i], to)

    def finish(self, level):
        self.drain()
        buf = self.slots[level]
        total = buf[0]
        for i in range(1, Place.sizes[self.groups[level]]):
            total = total + buf[i]
        return total


def kernel(
    frames,
    x_hbm, up_hbm, w1_hbm, b1, w2_hbm, b2,
    out_hbm, gin_hbm, gw1, gb1, gw2, gb2,
    xin, xc, up, hid, s1, g2, gh, g1, outb, ginb, pout, pin, tout, tin,
    w1, w2, w1t, w2t, acc1, acc2, db1, db2,
    *rest,
):
    nb = frames // R
    own = nb - 2
    bufs, rest = rest[:24], rest[24:]
    slots, rest = rest[:3], rest[3:]
    load_sem, out_sem, halo_send, halo_recv, ar_send, ar_recv, bias_send, bias_recv = rest

    place = Place()
    f, r = place.f, place.r
    n = lax.axis_size("frames")
    after = (lax.rem(f + 1, n), r)
    before = (lax.rem(f + n - 1, n), r)

    barrier = pltpu.get_barrier_semaphore()
    peers = [after, before] + [to for g in Place.sizes for _, to in place.others(g)]
    for peer in peers:
        pl.semaphore_signal(barrier, inc=1, device_id=peer, device_id_type=MESH)

    tail = 3 * R
    loads = [
        pltpu.make_async_copy(w1_hbm, w1, load_sem.at[0]),
        pltpu.make_async_copy(x_hbm.at[pl.ds(frames - tail, tail)], xin.at[pl.ds(HX + frames - tail, tail)], load_sem.at[1]),
        pltpu.make_async_copy(x_hbm.at[pl.ds(0, frames - tail)], xin.at[pl.ds(HX, frames - tail)], load_sem.at[2]),
        pltpu.make_async_copy(w2_hbm, w2, load_sem.at[3]),
        pltpu.make_async_copy(up_hbm, up, load_sem.at[4]),
    ]
    for copy in loads:
        copy.start()

    def halo(k, src, dst, to):
        return pltpu.make_async_remote_copy(
            src_ref=src, dst_ref=dst, send_sem=halo_send.at[k], recv_sem=halo_recv.at[k],
            device_id=to, device_id_type=MESH,
        )

    send_x1 = halo(0, xin.at[pl.ds(HX + frames - 1024, 1024)], xin.at[pl.ds(HX - 1024, 1024)], after)
    send_x2 = halo(1, xin.at[pl.ds(HX + frames - HX, HX - 1024)], xin.at[pl.ds(0, HX - 1024)], after)
    send_p = halo(2, pout, pin, after)
    send_g1 = halo(3, g1.at[pl.ds(0, 2 * D1)], g1.at[pl.ds(HH + own * R, 2 * D1)], before)
    send_t = halo(4, tout, tin, before)

    g2[pl.ds(0, HH), :] = jnp.zeros((HH, C), BF16)
    g2[pl.ds(HH + frames, HH), :] = jnp.zeros((HH, C), BF16)
    db1[...] = jnp.zeros_like(db1)
    db2[...] = jnp.zeros_like(db2)
    bias1 = b1[...].astype(F32).reshape(1, C)
    bias2 = b2[...].astype(F32).reshape(1, C)
    inner = jnp.where(f == 0, 0.0, 1.0).astype(F32)

    def rows(start, size=R):
        return pl.ds(start if isinstance(start, int) else pl.multiple_of(start, 256), size)

    def forward1(t, src, base, keep):
        x0 = src[rows(base + t), :]
        x1 = src[rows(base + t - D1), :]
        x2 = src[rows(base + t - 2 * D1), :]
        pre = dot(jnp.concatenate([x0, x1, x2], axis=1), w1[...]) + bias1
        act, slope = gelu_parts(pre)
        h = x0.astype(F32) + act
        hid[rows(t + HH), :] = (h if keep is None else h * keep).astype(BF16)
        s1[rows(t + HH), :] = slope

    def block_f1(b):
        forward1(b * R, xin, HX, None)

    def block_f2(b):
        t = b * R
        h = [hid[rows(t + HH - k * D2), :] for k in range(3)]
        pre = dot(jnp.concatenate(h, axis=1), w2[...]) + bias2
        act, slope = gelu_parts(pre)
        outb[rows(t), :] = (h[0].astype(F32) + act).astype(BF16)
        g = up[rows(t), :].astype(F32) * slope
        db2[...] += jnp.sum(g.reshape(R // 8, 8, C), axis=0)
        g2[rows(t + HH), :] = g.astype(BF16)
        out_copy(b).start()

    def hidden_terms(t):
        cat = jnp.concatenate([g2[rows(t + HH + k * D2), :] for k in range(3)], axis=1)
        return dot(cat, w2t[...])

    def backward2(t, grad):
        gh[rows(t + HH), :] = grad
        g = grad * s1[rows(t + HH), :]
        db1[...] += jnp.sum(g.reshape(R // 8, 8, C), axis=0)
        g1[rows(t + HH), :] = g.astype(BF16)

    def block_b2(b):
        t = b * R
        backward2(t, hidden_terms(t) + up[rows(t), :].astype(F32))

    def block_p(b):
        t = b * R
        pout[rows(t - own * R), :] = (hidden_terms(t) + up[rows(t), :].astype(F32)).astype(BF16)

    def block_b2_before(b):
        t = b * R
        backward2(t, pin[rows(t + HH), :].astype(F32) + inner * hidden_terms(t))

    def block_b1(b):
        t = b * R
        cat = jnp.concatenate([g1[rows(t + HH + k * D1), :] for k in range(3)], axis=1)
        ginb[rows(t), :] = (dot(cat, w1t[...]) + gh[rows(t + HH), :]).astype(BF16)
        gin_copy(b).start()

    def grad2(start, size, first=False):
        lhs = jnp.concatenate([hid[rows(start + HH - k * D2, size), :] for k in range(3)], axis=1)
        part = dot_rows(lhs, g2[rows(start + HH, size), :])
        acc2[...] = part if first else acc2[...] + part

    def grad1(start, size, first=False, src=None, base=HX):
        src = xin if src is None else src
        lhs = jnp.concatenate([src[rows(start + base - k * D1, size), :] for k in range(3)], axis=1)
        part = dot_rows(lhs, g1[rows(start + HH, size), :])
        acc1[...] = part if first else acc1[...] + part

    def out_copy(b):
        return pltpu.make_async_copy(outb.at[rows(b * R)], out_hbm.at[rows(b * R)], out_sem.at[b])

    def gin_copy(b):
        return pltpu.make_async_copy(ginb.at[rows(b * R)], gin_hbm.at[rows(b * R)], out_sem.at[nb + b])

    tail_copy = pltpu.make_async_copy(tin, gin_hbm.at[pl.ds(own * R, HH)], out_sem.at[nb + own])

    def loop(lo, hi, block):
        if hi - lo == 1:
            block(lo)
            return

        def body(b, _):
            block(b)
            return 0

        lax.fori_loop(lo, hi, body, 0)

    layer1 = Layer(place, bufs[:12], ar_send.at[0], ar_recv.at[0])
    layer2 = Layer(place, bufs[12:], ar_send.at[1], ar_recv.at[1])

    loads[0].wait()
    loads[1].wait()
    loop(nb - 2, nb, block_f1)
    pl.semaphore_wait(barrier, len(peers))
    send_x1.start()
    send_x2.start()
    loads[2].wait()
    loop(1, nb - 2, block_f1)
    loads[3].wait()
    loads[4].wait()
    for k in range(3):
        w1t[pl.ds(k * C, C), :] = w1[pl.ds(k * C, C), :].T
        w2t[pl.ds(k * C, C), :] = w2[pl.ds(k * C, C), :].T
    loop(3, nb, block_f2)
    loop(own, nb, block_p)
    send_p.start()
    loop(3, own, block_b2)
    grad2(frames - 1024, 1024, True)
    grad2(frames - 2048, 1024)
    grad1(own * R - 1024, 1024, True)
    grad1(own * R - 1536, 512)

    send_x1.wait()
    xc[pl.ds(0, R), :] = (xin[pl.ds(HX - R, R), :].astype(F32) * inner).astype(BF16)
    xc[pl.ds(R, R), :] = xin[pl.ds(HX, R), :]
    forward1(0, xc, R, None)
    forward1(-R, xin, HX, inner)
    loop(1, 3, block_f2)
    send_x2.wait()
    forward1(-2 * R, xin, HX, inner)
    loop(0, 1, block_f2)
    grad2(1024, 1024)
    grad2(0, 1024)
    layer2.begin(acc2)
    loop(0, 3, block_b2)
    layer2.step(1)
    grad1(0, R, False, xc, R)
    grad1(R, 1024)
    send_p.wait()
    block_b2_before(-2)
    send_g1.start()
    block_b2_before(-1)
    grad1(-1024, 1024)
    layer1.begin(acc1)
    bias = BiasSum(place, slots, bias_send, bias_recv)
    both = jnp.concatenate(
        [jnp.sum(v[...], axis=0, keepdims=True)[:, h * 128 : (h + 1) * 128] for v in (db2, db1) for h in range(2)]
        + [jnp.zeros((4, 128), F32)],
        axis=0,
    ) * (1.0 / 1024.0)
    bias.begin(0, both)
    layer2.step(2)

    cat = jnp.concatenate([g1[pl.ds(k * D1, R), :] for k in range(3)], axis=1)
    tout[pl.ds(0, R), :] = (dot(cat, w1t[...]) + gh[pl.ds(0, R), :]).astype(BF16)
    edge = (g1[pl.ds(HH, R), :].astype(F32) * inner).astype(BF16)
    cat = jnp.concatenate(
        [
            g1[pl.ds(R, R), :],
            jnp.concatenate([g1[pl.ds(R + D1, D1), :], edge[:D1]], axis=0),
            edge,
        ],
        axis=1,
    )
    tout[pl.ds(R, R), :] = (dot(cat, w1t[...]) + gh[pl.ds(R, R), :]).astype(BF16)
    layer1.step(1)
    bias.begin(1, bias.finish(0))
    send_t.start()
    loop(0, own - 1, block_b1)
    layer2.step(3)
    layer1.step(2)
    bias.begin(2, bias.finish(1))
    send_g1.wait()
    loop(own - 1, own, block_b1)
    layer2.step(4)
    layer1.step(3)
    total = bias.finish(2)
    for h in range(2):
        gb2[:, pl.ds(h * 128, 128)] = total[h : h + 1]
        gb1[:, pl.ds(h * 128, 128)] = total[2 + h : 3 + h]
    layer2.end(gw2)
    send_t.wait()
    tail_copy.start()
    layer1.step(4)
    for b in range(nb):
        out_copy(b).wait()
    for b in range(own):
        gin_copy(b).wait()
    tail_copy.wait()
    layer1.end(gw1)


def body(inputs, first_layer_weight, first_layer_bias, second_layer_weight, second_layer_bias, upstream):
    _, frames, c = inputs.shape
    any_spec = pl.BlockSpec(memory_space=pl.ANY)
    vmem = pl.BlockSpec(memory_space=pltpu.VMEM)
    nb = frames // R
    scratch = [
        pltpu.VMEM((HX + frames, C), BF16),
        pltpu.VMEM((2 * R, C), BF16),
        pltpu.VMEM((frames, C), BF16),
        pltpu.VMEM((HH + frames, C), BF16),
        pltpu.VMEM((HH + frames, C), F32),
        pltpu.VMEM((HH + frames + HH, C), BF16),
        pltpu.VMEM((frames, C), F32),
        pltpu.VMEM((frames + 2 * D1, C), BF16),
        pltpu.VMEM((frames, C), BF16),
        pltpu.VMEM((frames - HH, C), BF16),
        pltpu.VMEM((HH, C), BF16),
        pltpu.VMEM((HH, C), BF16),
        pltpu.VMEM((HH, C), BF16),
        pltpu.VMEM((HH, C), BF16),
        pltpu.VMEM((3 * C, C), BF16),
        pltpu.VMEM((3 * C, C), BF16),
        pltpu.VMEM((3 * C, C), BF16),
        pltpu.VMEM((3 * C, C), BF16),
        pltpu.VMEM((3 * C, C), F32),
        pltpu.VMEM((3 * C, C), F32),
        pltpu.VMEM((8, C), F32),
        pltpu.VMEM((8, C), F32),
    ]
    scratch += [pltpu.VMEM(s, BF16) for _ in range(2) for a, b in Layer.groups for s in Part.shapes(a, b)]
    scratch += [pltpu.VMEM((k, 8, 128), F32) for k in (2, 16, 8)]
    scratch += [
        pltpu.SemaphoreType.DMA((5,)),
        pltpu.SemaphoreType.DMA((2 * nb,)),
        pltpu.SemaphoreType.DMA((5,)),
        pltpu.SemaphoreType.DMA((5,)),
        pltpu.SemaphoreType.DMA((2, 2, Part.sems)),
        pltpu.SemaphoreType.DMA((2, 2, Part.sems)),
        pltpu.SemaphoreType.DMA((23,)),
        pltpu.SemaphoreType.DMA((23,)),
    ]
    outs = pl.pallas_call(
        functools.partial(kernel, frames),
        out_shape=[
            jax.ShapeDtypeStruct((frames, c), BF16),
            jax.ShapeDtypeStruct((frames, c), BF16),
            jax.ShapeDtypeStruct((3 * C, C), F32),
            jax.ShapeDtypeStruct((1, C), F32),
            jax.ShapeDtypeStruct((3 * C, C), F32),
            jax.ShapeDtypeStruct((1, C), F32),
        ],
        in_specs=[any_spec, any_spec, any_spec, vmem, any_spec, vmem],
        out_specs=[any_spec, any_spec, vmem, vmem, vmem, vmem],
        scratch_shapes=scratch,
        compiler_params=pltpu.CompilerParams(
            collective_id=0, has_side_effects=True, vmem_limit_bytes=56 * 1024 * 1024
        ),
    )(
        inputs.reshape(frames, c),
        upstream.reshape(frames, c),
        first_layer_weight.reshape(3 * C, C),
        first_layer_bias,
        second_layer_weight.reshape(3 * C, C),
        second_layer_bias,
    )
    out, gin, gw1, gb1, gw2, gb2 = outs
    return (
        out.reshape(1, frames, c),
        gin.reshape(1, frames, c),
        gw1.reshape(3, C, C),
        gb1.reshape(C),
        gw2.reshape(3, C, C),
        gb2.reshape(C),
    )


def solution(mesh):
    return jax.shard_map(
        body,
        mesh=mesh,
        in_specs=(P("runs", "frames", None), P(), P(), P(), P(), P("runs", "frames", None)),
        out_specs=(P("runs", "frames", None), P("runs", "frames", None), P(), P(), P(), P()),
        check_vma=False,
    )
```

time: 86.7 us -> 68.3 us (0.79)
  Pallas kernels: 75.7 us -> 59.7 us
  local copies, waits for them, and re-layouts: 10.2 us -> 7.74 us
    pallas_call x1, Pallas kernels: 75.7 us -> 59.7 us  [body(): pl.pallas_call(functools.partial(kernel, frames), out_shape=[jax.ShapeDty...]
    reshape x2 -> x0, local copies, waits for them, and re-layouts: 2.44 us -> none  [the longest x1 1.22 us: body(): first_layer_bias.reshape(1, C)]
where the time goes in v2:
time: 68.3 us; the launch traced here: 68.1 us
  Pallas kernels  59.7 us (87%)
  local copies, waits for them, and re-layouts  7.74 us (11%)
    pallas_call x1, Pallas kernels, body(): pl.pallas_call(functools.partial(kernel, frames), out_shape=[jax.ShapeDty...  59.7 us
    unnamed x16, local copies, waits for them, and re-layouts  7.74 us

profile of v2, /device:TPU:1, one launch (start us, length us, event | category | flops | bytes accessed | tf_op | source)
XLA Modules:
  0.0 68.1 jit_solution(1658530199892292586)
XLA Ops:
  0.6 59.7 %shard_map.109 = (bf16[4096,256]{1,0:T(8,128)(2,1)}, bf16[4096,256]{1,0:T(8,128)(2,1)}, f32[768,256]{1,0:T(8,128)}, f32[1,256]{1,0:T(1,128)}, f32[768,256]{1,0:T(8,128)}, /*index=5*/f32[1,256]{1,0:T(1,128)}) custom-call(bf16[4096,256]{1,0:T(8,128)(2,1)} %bitcast.10, bf16[4096,256]{1,0:T(8,128)(2,1)} %bitcast.11, bf16[768,256]{1,0:T(8,128)(2,1)} %bitcast.16, ...), custom_call_target="tpu_custom_call" | custom-call | tf_op jit(solution)/shard_map/pallas_call | solution.py:499
  60.4 0.0 copy-start
  60.4 3.2 %copy.18 = bf16[1,4096,256]{2,1,0:T(8,128)(2,1)} copy(bf16[1,4096,256]{2,1,0:T(8,128)(2,1)} %bitcast.13) | data formatting | bytes 4194304
  63.6 0.0 copy-done
  63.6 0.0 copy-start.2
  63.6 0.0 copy-start.4
  63.6 0.0 copy-start.1
  63.6 1.3 %copy.19 = bf16[1,4096,256]{2,1,0:T(8,128)(2,1)} copy(bf16[1,4096,256]{2,1,0:T(8,128)(2,1)S(1)} %bitcast.12) | data formatting | bytes 4194304
  64.9 0.3 copy-done.2
  65.2 0.0 copy-start.3
  65.2 0.9 %copy.20 = f32[3,256,256]{2,1,0:T(8,128)} copy(f32[3,256,256]{2,1,0:T(8,128)S(1)} %bitcast.15) | data formatting | bytes 1572864
  66.1 0.0 copy-done.4
  66.1 0.6 copy.21
  66.7 0.0 copy-done.1
  66.7 0.9 %copy.22 = f32[3,256,256]{2,1,0:T(8,128)} copy(f32[3,256,256]{2,1,0:T(8,128)S(1)} %bitcast.14) | data formatting | bytes 1572864
  67.6 0.0 copy-done.3
  67.6 0.6 copy.23
Async XLA Ops:
  60.4 3.2 %copy-start = (bf16[4096,256]{1,0:T(8,128)(2,1)S(1)}, bf16[4096,256]{1,0:T(8,128)(2,1)}, u32[]{:S(2)}) copy-start(bf16[4096,256]{1,0:T(8,128)(2,1)} %get-tuple-element.13) | copy-start | bytes 6291460
  63.6 1.7 %copy-start.2 = (f32[768,256]{1,0:T(8,128)S(1)}, f32[768,256]{1,0:T(8,128)}, u32[]{:S(2)}) copy-start(f32[768,256]{1,0:T(8,128)} %get-tuple-element.14) | copy-start | bytes 2359300
  63.6 2.5 %copy-start.4 = (f32[1,256]{1,0:T(1,128)S(1)}, f32[1,256]{1,0:T(1,128)}, u32[]{:S(2)}) copy-start(f32[1,256]{1,0:T(1,128)} %get-tuple-element.15) | copy-start | bytes 3076
  63.6 3.1 %copy-start.1 = (f32[768,256]{1,0:T(8,128)S(1)}, f32[768,256]{1,0:T(8,128)}, u32[]{:S(2)}) copy-start(f32[768,256]{1,0:T(8,128)} %get-tuple-element.16) | copy-start | bytes 2359300
  65.2 2.3 %copy-start.3 = (f32[1,256]{1,0:T(1,128)S(1)}, f32[1,256]{1,0:T(1,128)}, u32[]{:S(2)}) copy-start(f32[1,256]{1,0:T(1,128)} %get-tuple-element.17) | copy-start | bytes 3076

commit v3 on v2

--- a/solution.py
+++ b/solution.py
@@ -80,6 +80,7 @@
         self.p, self.send, self.recv = place, send, recv
         self.sem = 0
         self.open = []
+        self.sent = []
 
     def put(self, src, dst, to):
         copy = pltpu.make_async_remote_copy(
@@ -93,11 +94,16 @@
         self.sem += 1
         copy.start()
         self.open.append(copy)
+        self.sent.append(copy)
 
     def drain(self):
         for copy in self.open:
-            copy.wait()
+            copy.wait_recv()
         self.open = []
+
+    def finish_sends(self):
+        for copy in self.sent:
+            copy.wait_send()
 
 
 class Part(Sender):
@@ -114,7 +120,7 @@
         inner = (8, 2, 24, 128) if a == "xy" else (8, 24, 256)
         chunk = inner[-2:]
         n1 = Place.sizes[a]
-        return [(2,) + inner, inner, inner, (n1 - 1,) + chunk, (n2,) + chunk, (2,) + inner]
+        return [(2,) + inner, inner, inner, (n1 - 1,) + chunk, (n2,) + chunk], (2,) + inner
 
     def chunk(self, ref, lead, j):
         where = (j // 2, lax.rem(j, 2)) if self.a == "xy" else (j,)
@@ -165,21 +171,15 @@
             piece = acc[pl.ds(row, 384), :] * (1.0 / 1024.0)
             self.s0[...] = piece.reshape(2, 8, 24, 256).astype(BF16)
 
-    def unpack(self, out, row):
-        if self.a == "xy":
-            for h in range(2):
-                out[pl.ds(row, 384), pl.ds(h * 128, 128)] = self.fin[:, :, h].astype(F32).reshape(384, 128)
-        else:
-            out[pl.ds(row, 384), :] = self.fin[...].astype(F32).reshape(384, 256)
-
 
 class Layer:
     groups = (("xy", "z"), ("z", "xy"))
 
-    def __init__(self, place, refs, send, recv):
+    def __init__(self, place, refs, fins, send, recv):
         self.parts = []
         for q, (a, b) in enumerate(self.groups):
-            self.parts.append(Part(place, a, b, refs[q * 6 : q * 6 + 6], send.at[q], recv.at[q]))
+            own = tuple(refs[q * 5 : q * 5 + 5]) + (fins[q],)
+            self.parts.append(Part(place, a, b, own, send.at[q], recv.at[q]))
 
     def begin(self, acc):
         for q, part in enumerate(self.parts):
@@ -190,10 +190,13 @@
         for part in self.parts:
             getattr(part, "step%d" % k)()
 
-    def end(self, out):
-        for q, part in enumerate(self.parts):
+    def end(self):
+        for part in self.parts:
             part.drain()
-            part.unpack(out, q * 384)
+
+    def finish_sends(self):
+        for part in self.parts:
+            part.finish_sends()
 
 
 class BiasSum(Sender):
@@ -222,16 +225,16 @@
 def kernel(
     frames,
     x_hbm, up_hbm, w1_hbm, b1, w2_hbm, b2,
-    out_hbm, gin_hbm, gw1, gb1, gw2, gb2,
-    xin, xc, up, hid, s1, g2, gh, g1, outb, ginb, pout, pin, tout, tin,
+    outb, ginb, fin1a, fin1b, fin2a, fin2b, biases,
+    xin, xc, up, hid, s1, g2, gh, g1, pout, pin, tout,
     w1, w2, w1t, w2t, acc1, acc2, db1, db2,
     *rest,
 ):
     nb = frames // R
     own = nb - 2
-    bufs, rest = rest[:24], rest[24:]
+    bufs, rest = rest[:20], rest[20:]
     slots, rest = rest[:3], rest[3:]
-    load_sem, out_sem, halo_send, halo_recv, ar_send, ar_recv, bias_send, bias_recv = rest
+    load_sem, halo_send, halo_recv, ar_send, ar_recv, bias_send, bias_recv = rest
 
     place = Place()
     f, r = place.f, place.r
@@ -265,7 +268,7 @@
     send_x2 = halo(1, xin.at[pl.ds(HX + frames - HX, HX - 1024)], xin.at[pl.ds(0, HX - 1024)], after)
     send_p = halo(2, pout, pin, after)
     send_g1 = halo(3, g1.at[pl.ds(0, 2 * D1)], g1.at[pl.ds(HH + own * R, 2 * D1)], before)
-    send_t = halo(4, tout, tin, before)
+    send_t = halo(4, tout, ginb.at[pl.ds(own * R, HH)], before)
 
     g2[pl.ds(0, HH), :] = jnp.zeros((HH, C), BF16)
     g2[pl.ds(HH + frames, HH), :] = jnp.zeros((HH, C), BF16)
@@ -300,7 +303,6 @@
         g = up[rows(t), :].astype(F32) * slope
         db2[...] += jnp.sum(g.reshape(R // 8, 8, C), axis=0)
         g2[rows(t + HH), :] = g.astype(BF16)
-        out_copy(b).start()
 
     def hidden_terms(t):
         cat = jnp.concatenate([g2[rows(t + HH + k * D2), :] for k in range(3)], axis=1)
@@ -328,7 +330,6 @@
         t = b * R
         cat = jnp.concatenate([g1[rows(t + HH + k * D1), :] for k in range(3)], axis=1)
         ginb[rows(t), :] = (dot(cat, w1t[...]) + gh[rows(t + HH), :]).astype(BF16)
-        gin_copy(b).start()
 
     def grad2(start, size, first=False):
         lhs = jnp.concatenate([hid[rows(start + HH - k * D2, size), :] for k in range(3)], axis=1)
@@ -341,14 +342,6 @@
         part = dot_rows(lhs, g1[rows(start + HH, size), :])
         acc1[...] = part if first else acc1[...] + part
 
-    def out_copy(b):
-        return pltpu.make_async_copy(outb.at[rows(b * R)], out_hbm.at[rows(b * R)], out_sem.at[b])
-
-    def gin_copy(b):
-        return pltpu.make_async_copy(ginb.at[rows(b * R)], gin_hbm.at[rows(b * R)], out_sem.at[nb + b])
-
-    tail_copy = pltpu.make_async_copy(tin, gin_hbm.at[pl.ds(own * R, HH)], out_sem.at[nb + own])
-
     def loop(lo, hi, block):
         if hi - lo == 1:
             block(lo)
@@ -360,61 +353,62 @@
 
         lax.fori_loop(lo, hi, body, 0)
 
-    layer1 = Layer(place, bufs[:12], ar_send.at[0], ar_recv.at[0])
-    layer2 = Layer(place, bufs[12:], ar_send.at[1], ar_recv.at[1])
+    layer1 = Layer(place, bufs[:10], (fin1a, fin1b), ar_send.at[0], ar_recv.at[0])
+    layer2 = Layer(place, bufs[10:], (fin2a, fin2b), ar_send.at[1], ar_recv.at[1])
+    bias = BiasSum(place, slots, bias_send, bias_recv)
 
     loads[0].wait()
+    for k in range(3):
+        w1t[pl.ds(k * C, C), :] = w1[pl.ds(k * C, C), :].T
     loads[1].wait()
     loop(nb - 2, nb, block_f1)
+    loads[2].wait()
+    loop(1, nb - 2, block_f1)
+    loads[3].wait()
+    for k in range(3):
+        w2t[pl.ds(k * C, C), :] = w2[pl.ds(k * C, C), :].T
+    loads[4].wait()
     pl.semaphore_wait(barrier, len(peers))
     send_x1.start()
     send_x2.start()
-    loads[2].wait()
-    loop(1, nb - 2, block_f1)
-    loads[3].wait()
-    loads[4].wait()
-    for k in range(3):
-        w1t[pl.ds(k * C, C), :] = w1[pl.ds(k * C, C), :].T
-        w2t[pl.ds(k * C, C), :] = w2[pl.ds(k * C, C), :].T
-    loop(3, nb, block_f2)
+    loop(own, nb, block_f2)
     loop(own, nb, block_p)
     send_p.start()
+    loop(3, own, block_f2)
     loop(3, own, block_b2)
     grad2(frames - 1024, 1024, True)
     grad2(frames - 2048, 1024)
     grad1(own * R - 1024, 1024, True)
     grad1(own * R - 1536, 512)
 
-    send_x1.wait()
+    send_x1.wait_recv()
     xc[pl.ds(0, R), :] = (xin[pl.ds(HX - R, R), :].astype(F32) * inner).astype(BF16)
     xc[pl.ds(R, R), :] = xin[pl.ds(HX, R), :]
     forward1(0, xc, R, None)
     forward1(-R, xin, HX, inner)
     loop(1, 3, block_f2)
-    send_x2.wait()
+    send_x2.wait_recv()
     forward1(-2 * R, xin, HX, inner)
     loop(0, 1, block_f2)
+    loop(0, 3, block_b2)
     grad2(1024, 1024)
     grad2(0, 1024)
     layer2.begin(acc2)
-    loop(0, 3, block_b2)
-    layer2.step(1)
     grad1(0, R, False, xc, R)
     grad1(R, 1024)
-    send_p.wait()
+    layer2.step(1)
+    send_p.wait_recv()
     block_b2_before(-2)
     send_g1.start()
     block_b2_before(-1)
     grad1(-1024, 1024)
     layer1.begin(acc1)
-    bias = BiasSum(place, slots, bias_send, bias_recv)
     both = jnp.concatenate(
         [jnp.sum(v[...], axis=0, keepdims=True)[:, h * 128 : (h + 1) * 128] for v in (db2, db1) for h in range(2)]
         + [jnp.zeros((4, 128), F32)],
         axis=0,
     ) * (1.0 / 1024.0)
     bias.begin(0, both)
-    layer2.step(2)
 
     cat = jnp.concatenate([g1[pl.ds(k * D1, R), :] for k in range(3)], axis=1)
     tout[pl.ds(0, R), :] = (dot(cat, w1t[...]) + gh[pl.ds(0, R), :]).astype(BF16)
@@ -428,31 +422,45 @@
         axis=1,
     )
     tout[pl.ds(R, R), :] = (dot(cat, w1t[...]) + gh[pl.ds(R, R), :]).astype(BF16)
+    send_t.start()
     layer1.step(1)
     bias.begin(1, bias.finish(0))
-    send_t.start()
     loop(0, own - 1, block_b1)
-    layer2.step(3)
+    layer2.step(2)
+    send_g1.wait_recv()
+    loop(own - 1, own, block_b1)
     layer1.step(2)
     bias.begin(2, bias.finish(1))
-    send_g1.wait()
-    loop(own - 1, own, block_b1)
+    layer2.step(3)
+    layer1.step(3)
+    biases[...] = bias.finish(2)
     layer2.step(4)
-    layer1.step(3)
-    total = bias.finish(2)
+    layer1.step(4)
+    layer2.end()
+    send_t.wait_recv()
+    for copy in (send_x1, send_x2, send_p, send_g1, send_t):
+        copy.wait_send()
+    bias.finish_sends()
+    layer2.finish_sends()
+    layer1.finish_sends()
+    layer1.end()
+
+
+def write_kernel(outb, ginb, fin1a, fin1b, fin2a, fin2b, biases, out, gin, gw1, gb1, gw2, gb2, wide1, wide2, sem):
+    copies = [pltpu.make_async_copy(outb, out, sem.at[0]), pltpu.make_async_copy(ginb, gin, sem.at[1])]
+    for copy in copies:
+        copy.start()
+    for k, (a, b, wide, dst) in enumerate(((fin1a, fin1b, wide1, gw1), (fin2a, fin2b, wide2, gw2))):
+        for h in range(2):
+            wide[pl.ds(0, 384), pl.ds(h * 128, 128)] = a[:, :, h].astype(F32).reshape(384, 128)
+        wide[pl.ds(384, 384), :] = b[...].astype(F32).reshape(384, 256)
+        copies.append(pltpu.make_async_copy(wide, dst, sem.at[2 + k]))
+        copies[-1].start()
     for h in range(2):
-        gb2[:, pl.ds(h * 128, 128)] = total[h : h + 1]
-        gb1[:, pl.ds(h * 128, 128)] = total[2 + h : 3 + h]
-    layer2.end(gw2)
-    send_t.wait()
-    tail_copy.start()
-    layer1.step(4)
-    for b in range(nb):
-        out_copy(b).wait()
-    for b in range(own):
-        gin_copy(b).wait()
-    tail_copy.wait()
-    layer1.end(gw1)
+        gb2[:, pl.ds(h * 128, 128)] = biases[pl.ds(h, 1), :]
+        gb1[:, pl.ds(h * 128, 128)] = biases[pl.ds(2 + h, 1), :]
+    for copy in copies:
+        copy.wait()
 
 
 def body(inputs, first_layer_weight, first_layer_bias, second_layer_weight, second_layer_bias, upstream):
@@ -469,9 +477,6 @@
         pltpu.VMEM((HH + frames + HH, C), BF16),
         pltpu.VMEM((frames, C), F32),
         pltpu.VMEM((frames + 2 * D1, C), BF16),
-        pltpu.VMEM((frames, C), BF16),
-        pltpu.VMEM((frames - HH, C), BF16),
-        pltpu.VMEM((HH, C), BF16),
         pltpu.VMEM((HH, C), BF16),
         pltpu.VMEM((HH, C), BF16),
         pltpu.VMEM((HH, C), BF16),
@@ -484,11 +489,11 @@
         pltpu.VMEM((8, C), F32),
         pltpu.VMEM((8, C), F32),
     ]
-    scratch += [pltpu.VMEM(s, BF16) for _ in range(2) for a, b in Layer.groups for s in Part.shapes(a, b)]
+    scratch += [pltpu.VMEM(s, BF16) for _ in range(2) for a, b in Layer.groups for s in Part.shapes(a, b)[0]]
+    fins = [Part.shapes(a, b)[1] for _ in range(2) for a, b in Layer.groups]
     scratch += [pltpu.VMEM((k, 8, 128), F32) for k in (2, 16, 8)]
     scratch += [
         pltpu.SemaphoreType.DMA((5,)),
-        pltpu.SemaphoreType.DMA((2 * nb,)),
         pltpu.SemaphoreType.DMA((5,)),
         pltpu.SemaphoreType.DMA((5,)),
         pltpu.SemaphoreType.DMA((2, 2, Part.sems)),
@@ -496,21 +501,16 @@
         pltpu.SemaphoreType.DMA((23,)),
         pltpu.SemaphoreType.DMA((23,)),
     ]
-    outs = pl.pallas_call(
+    held = pl.pallas_call(
         functools.partial(kernel, frames),
-        out_shape=[
-            jax.ShapeDtypeStruct((frames, c), BF16),
-            jax.ShapeDtypeStruct((frames, c), BF16),
-            jax.ShapeDtypeStruct((3 * C, C), F32),
-            jax.ShapeDtypeStruct((1, C), F32),
-            jax.ShapeDtypeStruct((3 * C, C), F32),
-            jax.ShapeDtypeStruct((1, C), F32),
-        ],
+        out_shape=[pltpu.VMEM((frames, c), BF16)] * 2
+        + [pltpu.VMEM(shape, BF16) for shape in fins]
+        + [pltpu.VMEM((8, 128), F32)],
         in_specs=[any_spec, any_spec, any_spec, vmem, any_spec, vmem],
-        out_specs=[any_spec, any_spec, vmem, vmem, vmem, vmem],
+        out_specs=[vmem] * 7,
         scratch_shapes=scratch,
         compiler_params=pltpu.CompilerParams(
-            collective_id=0, has_side_effects=True, vmem_limit_bytes=56 * 1024 * 1024
+            collective_id=0, has_side_effects=True, vmem_limit_bytes=58 * 1024 * 1024
         ),
     )(
         inputs.reshape(frames, c),
@@ -520,6 +520,25 @@
         second_layer_weight.reshape(3 * C, C),
         second_layer_bias,
     )
+    outs = pl.pallas_call(
+        write_kernel,
+        out_shape=[
+            jax.ShapeDtypeStruct((frames, c), BF16),
+            jax.ShapeDtypeStruct((frames, c), BF16),
+            jax.ShapeDtypeStruct((3 * C, C), F32),
+            jax.ShapeDtypeStruct((1, C), F32),
+            jax.ShapeDtypeStruct((3 * C, C), F32),
+            jax.ShapeDtypeStruct((1, C), F32),
+        ],
+        in_specs=[vmem] * 7,
+        out_specs=[any_spec, any_spec, any_spec, vmem, any_spec, vmem],
+        scratch_shapes=[
+            pltpu.VMEM((3 * C, C), F32),
+            pltpu.VMEM((3 * C, C), F32),
+            pltpu.SemaphoreType.DMA((4,)),
+        ],
+        compiler_params=pltpu.CompilerParams(vmem_limit_bytes=8 * 1024 * 1024),
+    )(*held)
     out, gin, gw1, gb1, gw2, gb2 = outs
     return (
         out.reshape(1, frames, c),

time: 68.3 us -> 66.1 us (0.968)
  local copies, waits for them, and re-layouts: 7.74 us -> 0 us
  Pallas kernels: 59.7 us -> 65.4 us
    unnamed x16 -> x0, local copies, waits for them, and re-layouts: 7.74 us -> none
    pallas_call x1 -> x2, Pallas kernels: 59.7 us -> 65.4 us  [the longest x1 62.3 us: body(): pl.pallas_call(functools.partial(kernel, frames), out_shape=[pltpu.VMEM((...]
where the time goes in v3:
time: 66.1 us; the launch traced here: 66 us
  Pallas kernels  65.4 us (99%)
    pallas_call x1, Pallas kernels, body(): pl.pallas_call(functools.partial(kernel, frames), out_shape=[pltpu.VMEM((...  62.3 us
    pallas_call x1, Pallas kernels, body(): pl.pallas_call(write_kernel, out_shape=[jax.ShapeDtypeStruct((frames, c),...  3.1 us

profile of v3, /device:TPU:1, one launch (start us, length us, event | category | flops | bytes accessed | tf_op | source)
XLA Modules:
  0.0 66.0 jit_solution(5869815868704072008)
XLA Ops:
  0.6 62.3 %shard_map.109 = (bf16[4096,256]{1,0:T(8,128)(2,1)S(1)}, bf16[4096,256]{1,0:T(8,128)(2,1)S(1)}, bf16[2,8,2,24,128]{4,3,2,1,0:T(8,128)(2,1)S(1)}, bf16[2,8,24,256...) custom-call(bf16[4096,256]{1,0:T(8,128)(2,1)} %bitcast.10, ...), custom_call_target="tpu_custom_call" | custom-call | tf_op jit(solution)/shard_map/pallas_call | solution.py:504
  62.9 3.1 %shard_map.110 = (bf16[4096,256]{1,0:T(8,128)(2,1)}, bf16[4096,256]{1,0:T(8,128)(2,1)}, f32[768,256]{1,0:T(8,128)}, f32[1,256]{1,0:T(1,128)}, f32[768,256]{1,0:T(8,128)}, /*index=5*/f32[1,256]{1,0:T(1,128)}) custom-call(bf16[4096,256]{1,0:T(8,128)(2,1)S(1)} %get-tuple-element.19.outb, bf16[4096,256]{1,0:T(8,128)(2,1)S(1)} %get-tuple-element.20.ginb, ...), custom_call_target="tpu_custom_call" | custom-call | tf_op jit(solution)/shard_map/pallas_call | solution.py:523

commit v4 on v3

--- a/solution.py
+++ b/solution.py
@@ -14,7 +14,7 @@
 D2 = 512
 HX = 1536
 HH = 1024
-R = 512
+R = 1024
 F32 = jnp.float32
 BF16 = jnp.bfloat16
 C0 = math.sqrt(2.0 / math.pi)
@@ -231,7 +231,7 @@
     *rest,
 ):
     nb = frames // R
-    own = nb - 2
+    own = nb - 1
     bufs, rest = rest[:20], rest[20:]
     slots, rest = rest[:3], rest[3:]
     load_sem, halo_send, halo_recv, ar_send, ar_recv, bias_send, bias_recv = rest
@@ -247,13 +247,14 @@
     for peer in peers:
         pl.semaphore_signal(barrier, inc=1, device_id=peer, device_id_type=MESH)
 
-    tail = 3 * R
+    tail = HX
     loads = [
         pltpu.make_async_copy(w1_hbm, w1, load_sem.at[0]),
         pltpu.make_async_copy(x_hbm.at[pl.ds(frames - tail, tail)], xin.at[pl.ds(HX + frames - tail, tail)], load_sem.at[1]),
         pltpu.make_async_copy(x_hbm.at[pl.ds(0, frames - tail)], xin.at[pl.ds(HX, frames - tail)], load_sem.at[2]),
         pltpu.make_async_copy(w2_hbm, w2, load_sem.at[3]),
         pltpu.make_async_copy(up_hbm, up, load_sem.at[4]),
+        pltpu.make_async_copy(x_hbm.at[pl.ds(0, 2 * R)], xc.at[pl.ds(2 * D1, 2 * R)], load_sem.at[5]),
     ]
     for copy in loads:
         copy.start()
@@ -322,10 +323,6 @@
         t = b * R
         pout[rows(t - own * R), :] = (hidden_terms(t) + up[rows(t), :].astype(F32)).astype(BF16)
 
-    def block_b2_before(b):
-        t = b * R
-        backward2(t, pin[rows(t + HH), :].astype(F32) + inner * hidden_terms(t))
-
     def block_b1(b):
         t = b * R
         cat = jnp.concatenate([g1[rows(t + HH + k * D1), :] for k in range(3)], axis=1)
@@ -358,50 +355,44 @@
     bias = BiasSum(place, slots, bias_send, bias_recv)
 
     loads[0].wait()
-    for k in range(3):
-        w1t[pl.ds(k * C, C), :] = w1[pl.ds(k * C, C), :].T
     loads[1].wait()
-    loop(nb - 2, nb, block_f1)
-    loads[2].wait()
-    loop(1, nb - 2, block_f1)
-    loads[3].wait()
-    for k in range(3):
-        w2t[pl.ds(k * C, C), :] = w2[pl.ds(k * C, C), :].T
-    loads[4].wait()
+    block_f1(3)
     pl.semaphore_wait(barrier, len(peers))
     send_x1.start()
     send_x2.start()
-    loop(own, nb, block_f2)
-    loop(own, nb, block_p)
+    loads[2].wait()
+    loop(1, 3, block_f1)
+    loads[3].wait()
+    loads[4].wait()
+    for k in range(3):
+        w2t[pl.ds(k * C, C), :] = w2[pl.ds(k * C, C), :].T
+    block_f2(3)
+    block_p(3)
     send_p.start()
-    loop(3, own, block_f2)
-    loop(3, own, block_b2)
-    grad2(frames - 1024, 1024, True)
-    grad2(frames - 2048, 1024)
-    grad1(own * R - 1024, 1024, True)
-    grad1(own * R - 1536, 512)
-
+    block_f2(2)
+    block_b2(2)
+    grad2(2 * R, 2 * R, True)
+    grad1(2 * R, R, True)
+    for k in range(3):
+        w1t[pl.ds(k * C, C), :] = w1[pl.ds(k * C, C), :].T
+
+    loads[5].wait()
     send_x1.wait_recv()
-    xc[pl.ds(0, R), :] = (xin[pl.ds(HX - R, R), :].astype(F32) * inner).astype(BF16)
-    xc[pl.ds(R, R), :] = xin[pl.ds(HX, R), :]
-    forward1(0, xc, R, None)
+    xc[pl.ds(0, 2 * D1), :] = (xin[pl.ds(HX - 2 * D1, 2 * D1), :].astype(F32) * inner).astype(BF16)
+    forward1(0, xc, 2 * D1, None)
+    block_f2(1)
+    send_x2.wait_recv()
     forward1(-R, xin, HX, inner)
-    loop(1, 3, block_f2)
-    send_x2.wait_recv()
-    forward1(-2 * R, xin, HX, inner)
-    loop(0, 1, block_f2)
-    loop(0, 3, block_b2)
-    grad2(1024, 1024)
-    grad2(0, 1024)
+    block_f2(0)
+    loop(0, 2, block_b2)
+    grad2(0, 2 * R)
     layer2.begin(acc2)
-    grad1(0, R, False, xc, R)
-    grad1(R, 1024)
+    grad1(0, 2 * R, False, xc, 2 * D1)
     layer2.step(1)
     send_p.wait_recv()
-    block_b2_before(-2)
+    backward2(-R, pin[...].astype(F32) + inner * hidden_terms(-R))
     send_g1.start()
-    block_b2_before(-1)
-    grad1(-1024, 1024)
+    grad1(-R, R)
     layer1.begin(acc1)
     both = jnp.concatenate(
         [jnp.sum(v[...], axis=0, keepdims=True)[:, h * 128 : (h + 1) * 128] for v in (db2, db1) for h in range(2)]
@@ -410,18 +401,16 @@
     ) * (1.0 / 1024.0)
     bias.begin(0, both)
 
-    cat = jnp.concatenate([g1[pl.ds(k * D1, R), :] for k in range(3)], axis=1)
-    tout[pl.ds(0, R), :] = (dot(cat, w1t[...]) + gh[pl.ds(0, R), :]).astype(BF16)
-    edge = (g1[pl.ds(HH, R), :].astype(F32) * inner).astype(BF16)
+    edge = (g1[pl.ds(HH, 2 * D1), :].astype(F32) * inner).astype(BF16)
     cat = jnp.concatenate(
         [
-            g1[pl.ds(R, R), :],
-            jnp.concatenate([g1[pl.ds(R + D1, D1), :], edge[:D1]], axis=0),
-            edge,
+            g1[pl.ds(0, R), :],
+            jnp.concatenate([g1[pl.ds(D1, R - D1), :], edge[:D1]], axis=0),
+            jnp.concatenate([g1[pl.ds(2 * D1, R - 2 * D1), :], edge], axis=0),
         ],
         axis=1,
     )
-    tout[pl.ds(R, R), :] = (dot(cat, w1t[...]) + gh[pl.ds(R, R), :]).astype(BF16)
+    tout[...] = (dot(cat, w1t[...]) + gh[pl.ds(0, R), :]).astype(BF16)
     send_t.start()
     layer1.step(1)
     bias.begin(1, bias.finish(0))
@@ -470,7 +459,7 @@
     nb = frames // R
     scratch = [
         pltpu.VMEM((HX + frames, C), BF16),
-        pltpu.VMEM((2 * R, C), BF16),
+        pltpu.VMEM((2 * R + 2 * D1, C), BF16),
         pltpu.VMEM((frames, C), BF16),
         pltpu.VMEM((HH + frames, C), BF16),
         pltpu.VMEM((HH + frames, C), F32),
@@ -493,7 +482,7 @@
     fins = [Part.shapes(a, b)[1] for _ in range(2) for a, b in Layer.groups]
     scratch += [pltpu.VMEM((k, 8, 128), F32) for k in (2, 16, 8)]
     scratch += [
-        pltpu.SemaphoreType.DMA((5,)),
+        pltpu.SemaphoreType.DMA((6,)),
         pltpu.SemaphoreType.DMA((5,)),
         pltpu.SemaphoreType.DMA((5,)),
         pltpu.SemaphoreType.DMA((2, 2, Part.sems)),

time: 66.1 us -> 64.9 us (0.982)
  Pallas kernels: 65.4 us -> 64 us
    pallas_call x1, Pallas kernels: 62.3 us -> 60.9 us  [body(): pl.pallas_call(functools.partial(kernel, frames), out_shape=[pltpu.VMEM((...]
where the time goes in v4:
time: 64.9 us; the launch traced here: 64.8 us
  Pallas kernels  64 us (99%)
  between operations  0.8 us (1%)
    pallas_call x1, Pallas kernels, body(): pl.pallas_call(functools.partial(kernel, frames), out_shape=[pltpu.VMEM((...  60.9 us
    pallas_call x1, Pallas kernels, body(): pl.pallas_call(write_kernel, out_shape=[jax.ShapeDtypeStruct((frames, c),...  3.1 us

profile of v4, /device:TPU:1, one launch (start us, length us, event | category | flops | bytes accessed | tf_op | source)
XLA Modules:
  0.0 64.8 jit_solution(14011258904510016720)
XLA Ops:
  0.6 60.9 %shard_map.109 = (bf16[4096,256]{1,0:T(8,128)(2,1)S(1)}, bf16[4096,256]{1,0:T(8,128)(2,1)S(1)}, bf16[2,8,2,24,128]{4,3,2,1,0:T(8,128)(2,1)S(1)}, bf16[2,8,24,256...) custom-call(bf16[4096,256]{1,0:T(8,128)(2,1)} %bitcast.10, ...), custom_call_target="tpu_custom_call" | custom-call | tf_op jit(solution)/shard_map/pallas_call | solution.py:493
  61.5 3.1 %shard_map.110 = (bf16[4096,256]{1,0:T(8,128)(2,1)}, bf16[4096,256]{1,0:T(8,128)(2,1)}, f32[768,256]{1,0:T(8,128)}, f32[1,256]{1,0:T(1,128)}, f32[768,256]{1,0:T(8,128)}, /*index=5*/f32[1,256]{1,0:T(1,128)}) custom-call(bf16[4096,256]{1,0:T(8,128)(2,1)S(1)} %get-tuple-element.19.outb, bf16[4096,256]{1,0:T(8,128)(2,1)S(1)} %get-tuple-element.20.ginb, ...), custom_call_target="tpu_custom_call" | custom-call | tf_op jit(solution)/shard_map/pallas_call | solution.py:512

commit v5 on v4

--- a/solution.py
+++ b/solution.py
@@ -226,7 +226,7 @@
     frames,
     x_hbm, up_hbm, w1_hbm, b1, w2_hbm, b2,
     outb, ginb, fin1a, fin1b, fin2a, fin2b, biases,
-    xin, xc, up, hid, s1, g2, gh, g1, pout, pin, tout,
+    xin, xc, up, hid, s1, g2, g2h, gh, g1, pout, pin,
     w1, w2, w1t, w2t, acc1, acc2, db1, db2,
     *rest,
 ):
@@ -268,8 +268,10 @@
     send_x1 = halo(0, xin.at[pl.ds(HX + frames - 1024, 1024)], xin.at[pl.ds(HX - 1024, 1024)], after)
     send_x2 = halo(1, xin.at[pl.ds(HX + frames - HX, HX - 1024)], xin.at[pl.ds(0, HX - 1024)], after)
     send_p = halo(2, pout, pin, after)
-    send_g1 = halo(3, g1.at[pl.ds(0, 2 * D1)], g1.at[pl.ds(HH + own * R, 2 * D1)], before)
-    send_t = halo(4, tout, ginb.at[pl.ds(own * R, HH)], before)
+    send_g2 = [halo(3 + i, g2.at[pl.ds(HH + i * D1, D1)], g2h.at[pl.ds(i * D1, D1)], before) for i in range(4)]
+    send_g1 = [
+        halo(7 + i, g1.at[pl.ds(HH + i * D1, D1)], g1.at[pl.ds(HH + frames + i * D1, D1)], before) for i in range(2)
+    ]
 
     g2[pl.ds(0, HH), :] = jnp.zeros((HH, C), BF16)
     g2[pl.ds(HH + frames, HH), :] = jnp.zeros((HH, C), BF16)
@@ -278,6 +280,7 @@
     bias1 = b1[...].astype(F32).reshape(1, C)
     bias2 = b2[...].astype(F32).reshape(1, C)
     inner = jnp.where(f == 0, 0.0, 1.0).astype(F32)
+    outer = jnp.where(f == n - 1, 0.0, 1.0).astype(F32)
 
     def rows(start, size=R):
         return pl.ds(start if isinstance(start, int) else pl.multiple_of(start, 256), size)
@@ -309,11 +312,20 @@
         cat = jnp.concatenate([g2[rows(t + HH + k * D2), :] for k in range(3)], axis=1)
         return dot(cat, w2t[...])
 
-    def backward2(t, grad):
-        gh[rows(t + HH), :] = grad
+    def backward2(t, grad, summed=True):
+        if not (isinstance(t, int) and t < 0):
+            gh[rows(t), :] = grad
         g = grad * s1[rows(t + HH), :]
-        db1[...] += jnp.sum(g.reshape(R // 8, 8, C), axis=0)
+        if summed:
+            db1[...] += jnp.sum(g.reshape(R // 8, 8, C), axis=0)
         g1[rows(t + HH), :] = g.astype(BF16)
+
+    def block_b2_last():
+        t = frames - R
+        near, far = g2[rows(t + HH), :], g2h[...]
+        mixed = jnp.concatenate([g2[rows(t + HH + D2, R - D2), :], far[:D2]], axis=0)
+        terms = dot(jnp.concatenate([near, mixed, far], axis=1), w2t[...])
+        backward2(t, terms + up[rows(t), :].astype(F32), False)
 
     def block_b2(b):
         t = b * R
@@ -326,7 +338,7 @@
     def block_b1(b):
         t = b * R
         cat = jnp.concatenate([g1[rows(t + HH + k * D1), :] for k in range(3)], axis=1)
-        ginb[rows(t), :] = (dot(cat, w1t[...]) + gh[rows(t + HH), :]).astype(BF16)
+        ginb[rows(t), :] = (dot(cat, w1t[...]) + gh[rows(t), :]).astype(BF16)
 
     def grad2(start, size, first=False):
         lhs = jnp.concatenate([hid[rows(start + HH - k * D2, size), :] for k in range(3)], axis=1)
@@ -384,14 +396,19 @@
     send_x2.wait_recv()
     forward1(-R, xin, HX, inner)
     block_f2(0)
-    loop(0, 2, block_b2)
+    send_g2[0].start()
+    send_g2[1].start()
+    block_b2(1)
+    block_b2(0)
+    send_g2[2].start()
     grad2(0, 2 * R)
     layer2.begin(acc2)
+    send_g2[3].start()
     grad1(0, 2 * R, False, xc, 2 * D1)
     layer2.step(1)
+    send_g1[0].start()
     send_p.wait_recv()
     backward2(-R, pin[...].astype(F32) + inner * hidden_terms(-R))
-    send_g1.start()
     grad1(-R, R)
     layer1.begin(acc1)
     both = jnp.concatenate(
@@ -400,24 +417,21 @@
         axis=0,
     ) * (1.0 / 1024.0)
     bias.begin(0, both)
-
-    edge = (g1[pl.ds(HH, 2 * D1), :].astype(F32) * inner).astype(BF16)
-    cat = jnp.concatenate(
-        [
-            g1[pl.ds(0, R), :],
-            jnp.concatenate([g1[pl.ds(D1, R - D1), :], edge[:D1]], axis=0),
-            jnp.concatenate([g1[pl.ds(2 * D1, R - 2 * D1), :], edge], axis=0),
-        ],
-        axis=1,
-    )
-    tout[...] = (dot(cat, w1t[...]) + gh[pl.ds(0, R), :]).astype(BF16)
-    send_t.start()
+    send_g1[1].start()
+    loop(0, 2, block_b1)
     layer1.step(1)
     bias.begin(1, bias.finish(0))
-    loop(0, own - 1, block_b1)
+    for copy in send_g2:
+        copy.wait_recv()
+    g2h[...] = (g2h[...].astype(F32) * outer).astype(BF16)
+    block_b2_last()
+    block_b1(2)
     layer2.step(2)
-    send_g1.wait_recv()
-    loop(own - 1, own, block_b1)
+    for copy in send_g1:
+        copy.wait_recv()
+    edge = pl.ds(HH + frames, 2 * D1)
+    g1[edge, :] = (g1[edge, :].astype(F32) * outer).astype(BF16)
+    block_b1(3)
     layer1.step(2)
     bias.begin(2, bias.finish(1))
     layer2.step(3)
@@ -426,8 +440,7 @@
     layer2.step(4)
     layer1.step(4)
     layer2.end()
-    send_t.wait_recv()
-    for copy in (send_x1, send_x2, send_p, send_g1, send_t):
+    for copy in [send_x1, send_x2, send_p] + send_g2 + send_g1:
         copy.wait_send()
     bias.finish_sends()
     layer2.finish_sends()
@@ -464,9 +477,9 @@
         pltpu.VMEM((HH + frames, C), BF16),
         pltpu.VMEM((HH + frames, C), F32),
         pltpu.VMEM((HH + frames + HH, C), BF16),
+        pltpu.VMEM((HH, C), BF16),
         pltpu.VMEM((frames, C), F32),
-        pltpu.VMEM((frames + 2 * D1, C), BF16),
-        pltpu.VMEM((HH, C), BF16),
+        pltpu.VMEM((HH + frames + 2 * D1, C), BF16),
         pltpu.VMEM((HH, C), BF16),
         pltpu.VMEM((HH, C), BF16),
         pltpu.VMEM((3 * C, C), BF16),
@@ -483,8 +496,8 @@
     scratch += [pltpu.VMEM((k, 8, 128), F32) for k in (2, 16, 8)]
     scratch += [
         pltpu.SemaphoreType.DMA((6,)),
-        pltpu.SemaphoreType.DMA((5,)),
-        pltpu.SemaphoreType.DMA((5,)),
+        pltpu.SemaphoreType.DMA((9,)),
+        pltpu.SemaphoreType.DMA((9,)),
         pltpu.SemaphoreType.DMA((2, 2, Part.sems)),
         pltpu.SemaphoreType.DMA((2, 2, Part.sems)),
         pltpu.SemaphoreType.DMA((23,)),

time: 64.9 us -> 60.2 us (0.928)
  Pallas kernels: 64 us -> 59.3 us
    pallas_call x1, Pallas kernels: 60.9 us -> 56.2 us  [body(): pl.pallas_call(functools.partial(kernel, frames), out_shape=[pltpu.VMEM((...]
where the time goes in v5:
time: 60.2 us; the launch traced here: 60.1 us
  Pallas kernels  59.3 us (99%)
  between operations  0.82 us (1%)
    pallas_call x1, Pallas kernels, body(): pl.pallas_call(functools.partial(kernel, frames), out_shape=[pltpu.VMEM((...  56.2 us
    pallas_call x1, Pallas kernels, body(): pl.pallas_call(write_kernel, out_shape=[jax.ShapeDtypeStruct((frames, c),...  3.1 us

profile of v5, /device:TPU:1, one launch (start us, length us, event | category | flops | bytes accessed | tf_op | source)
XLA Modules:
  0.0 60.1 jit_solution(4667683991781695750)
XLA Ops:
  0.6 56.2 %shard_map.109 = (bf16[4096,256]{1,0:T(8,128)(2,1)S(1)}, bf16[4096,256]{1,0:T(8,128)(2,1)S(1)}, bf16[2,8,2,24,128]{4,3,2,1,0:T(8,128)(2,1)S(1)}, bf16[2,8,24,256...) custom-call(bf16[4096,256]{1,0:T(8,128)(2,1)} %bitcast.10, ...), custom_call_target="tpu_custom_call" | custom-call | tf_op jit(solution)/shard_map/pallas_call | solution.py:506
  56.9 3.1 %shard_map.110 = (bf16[4096,256]{1,0:T(8,128)(2,1)}, bf16[4096,256]{1,0:T(8,128)(2,1)}, f32[768,256]{1,0:T(8,128)}, f32[1,256]{1,0:T(1,128)}, f32[768,256]{1,0:T(8,128)}, /*index=5*/f32[1,256]{1,0:T(1,128)}) custom-call(bf16[4096,256]{1,0:T(8,128)(2,1)S(1)} %get-tuple-element.19.outb, bf16[4096,256]{1,0:T(8,128)(2,1)S(1)} %get-tuple-element.20.ginb, ...), custom_call_target="tpu_custom_call" | custom-call | tf_op jit(solution)/shard_map/pallas_call | solution.py:525

commit v6 on v5

--- a/solution.py
+++ b/solution.py
@@ -25,10 +25,9 @@
 def gelu_parts(v):
     v2 = v * v
     t = jnp.tanh(v * (C0 + C1 * v2))
-    h = 0.5 * v
-    act = h + h * t
-    slope = (0.5 + 0.5 * t) + (h * (1.0 - t * t)) * (C0 + (3.0 * C1) * v2)
-    return act, slope
+    s = 0.5 + 0.5 * t
+    slope = s + (s - s * t) * (v * (C0 + (3.0 * C1) * v2))
+    return v * s, slope
 
 
 def dot(a, b):
@@ -385,8 +384,6 @@
     block_b2(2)
     grad2(2 * R, 2 * R, True)
     grad1(2 * R, R, True)
-    for k in range(3):
-        w1t[pl.ds(k * C, C), :] = w1[pl.ds(k * C, C), :].T
 
     loads[5].wait()
     send_x1.wait_recv()
@@ -418,6 +415,8 @@
     ) * (1.0 / 1024.0)
     bias.begin(0, both)
     send_g1[1].start()
+    for k in range(3):
+        w1t[pl.ds(k * C, C), :] = w1[pl.ds(k * C, C), :].T
     loop(0, 2, block_b1)
     layer1.step(1)
     bias.begin(1, bias.finish(0))

time: 60.2 us -> 59.8 us (level)
  no operation moved by 1% of the time
where the time goes in v6:
time: 59.8 us; the launch traced here: 59.7 us
  Pallas kernels  58.9 us (98%)
  between operations  0.82 us (1%)
    pallas_call x1, Pallas kernels, body(): pl.pallas_call(functools.partial(kernel, frames), out_shape=[pltpu.VMEM((...  55.8 us
    pallas_call x1, Pallas kernels, body(): pl.pallas_call(write_kernel, out_shape=[jax.ShapeDtypeStruct((frames, c),...  3.1 us

profile of v6, /device:TPU:1, one launch (start us, length us, event | category | flops | bytes accessed | tf_op | source)
XLA Modules:
  0.0 59.7 jit_solution(7658603388263271743)
XLA Ops:
  0.6 55.8 %shard_map.109 = (bf16[4096,256]{1,0:T(8,128)(2,1)S(1)}, bf16[4096,256]{1,0:T(8,128)(2,1)S(1)}, bf16[2,8,2,24,128]{4,3,2,1,0:T(8,128)(2,1)S(1)}, bf16[2,8,24,256...) custom-call(bf16[4096,256]{1,0:T(8,128)(2,1)} %bitcast.10, ...), custom_call_target="tpu_custom_call" | custom-call | tf_op jit(solution)/shard_map/pallas_call | solution.py:505
  56.4 3.1 %shard_map.110 = (bf16[4096,256]{1,0:T(8,128)(2,1)}, bf16[4096,256]{1,0:T(8,128)(2,1)}, f32[768,256]{1,0:T(8,128)}, f32[1,256]{1,0:T(1,128)}, f32[768,256]{1,0:T(8,128)}, /*index=5*/f32[1,256]{1,0:T(1,128)}) custom-call(bf16[4096,256]{1,0:T(8,128)(2,1)S(1)} %get-tuple-element.19.outb, bf16[4096,256]{1,0:T(8,128)(2,1)S(1)} %get-tuple-element.20.ginb, ...), custom_call_target="tpu_custom_call" | custom-call | tf_op jit(solution)/shard_map/pallas_call | solution.py:524
